TPU v7x, 256 devices: a whole 4x4x8 slice. The times are simulated.
256 devices in a mesh: dst: 32 (over y, z), src: 8 (over x, core).
Axes of the slice: x: 4, y: 4, z: 8, core: 2. Of those that a mesh axis runs over, the one named last changes fastest.
Arguments:
- transitions: bfloat16 [16384, 128, 128], P(('dst', 'src')), may hold values from 0.0009994507 to 1
- row_block: int32 [16384], P(('dst', 'src')), may hold values from -1 to 1023, as said below
- col_block: int32 [16384], P(('dst', 'src')), may hold values from -1 to 1023, as said below
- beta_last: float32 [32, 128, 8, 128], P(None, 'dst', 'src'), may hold values from 0.2 to 2
- emissions: bfloat16 [2, 32, 128, 8, 128], P(None, None, 'dst', 'src'), may hold values from 0.019897461 to 1
- forward: bfloat16 [2, 32, 128, 8, 128], P(None, None, 'dst', 'src'), may hold values from 0.03 to 125, as said below
Outputs:
- counts: bfloat16 [16384, 128, 128], P(('dst', 'src'))
- beta_first: float32 [32, 128, 8, 128], P(None, 'dst', 'src')
- log_norms: float32 [2, 32], replicated
Inputs may be any that keep to these rules, and one draw needn't show every extreme that they name: `row_block`: slots are grouped by device (index dst * 8 + src), 64 to a device. A live slot holds a block whose source block number r has r % 8 equal to the device's src index and whose destination block lies in the device's dst index's own consecutive equal share of blocks; no block appears twice; live slots come first, and empty ones hold -1 in both arrays. One device has all 64 slots live; each device has at least one. `col_block`: same slots as row_block; -1 exactly where row_block is -1. `forward`: Positive.
All inputs are finite; a program needn't handle non-finite values.
Results may differ from a plain program's by a relative error of at most 0.0029.
Values may be sent and summed in bfloat16 or wider, within the bound.
No kernel may reach another device: no remote copies, remote signals or barrier semaphores. Data moves between devices by JAX's collectives and lax.ppermute only.
A program may use at most 64 MiB of HBM per device.

v0:
```python
import jax
import jax.numpy as jnp
from jax import lax
from jax.sharding import PartitionSpec as P

S = 131072
STEPS = 2


def body(transitions, row_block, col_block, beta_last, emissions, forward):
    source_count = lax.axis_size("src")
    seq_count = beta_last.shape[0]
    local_rows = beta_last.shape[1]
    block_size = beta_last.shape[3]
    slot_count = transitions.shape[0]
    column_count = local_rows * source_count
    total_rows = local_rows * lax.axis_size("dst")
    living = row_block >= 0
    live_float = living.astype(jnp.float32)
    row_local = jnp.where(living, row_block // source_count, 0)
    col_local = jnp.where(living, col_block % column_count, 0)
    beta_piece = beta_last[:, :, 0, :]
    count_sum = jnp.zeros((slot_count, block_size, block_size), jnp.float32)
    log_list = []
    for step_index in range(STEPS):
        emitted = emissions[step_index][:, :, 0, :]
        message = (emitted.astype(jnp.float32) * beta_piece).astype(jnp.bfloat16)
        columns = lax.all_gather(message[:, :, None, :], "src", axis=2, tiled=True)
        columns = columns.reshape(seq_count, column_count, block_size)
        alpha_rows = lax.all_gather(forward[step_index], "dst", axis=1, tiled=True)
        alpha_rows = alpha_rows.reshape(seq_count, total_rows, block_size)
        alpha_picked = jnp.take(alpha_rows, row_local, axis=1)
        picked = jnp.take(columns, col_local, axis=1)
        products = jnp.einsum(
            "bcj,cij->cbi", picked, transitions, preferred_element_type=jnp.float32
        )
        products = products * live_float[:, None, None]
        partial_value = jax.ops.segment_sum(products, row_local, num_segments=total_rows)
        raw_sums = lax.psum_scatter(partial_value, "dst", scatter_dimension=0, tiled=True)
        own_alpha = forward[step_index][:, :, 0, :]
        local_term = jnp.einsum(
            "kbr,bkr->b", raw_sums, own_alpha, preferred_element_type=jnp.float32
        )
        scale_now = lax.psum(local_term, ("dst", "src")) / S
        beta_piece = jnp.transpose(raw_sums / scale_now[None, :, None], (1, 0, 2))
        scaled = (columns.astype(jnp.float32) / scale_now[:, None, None]).astype(jnp.bfloat16)
        scaled_picked = jnp.take(scaled, col_local, axis=1)
        count_sum = count_sum + jnp.einsum(
            "bci,bcj->cij", alpha_picked, scaled_picked, preferred_element_type=jnp.float32
        )
        log_list.append(jnp.log(scale_now))
    counts = (count_sum * transitions.astype(jnp.float32) * live_float[:, None, None]).astype(
        jnp.bfloat16
    )
    return (counts, beta_piece[:, :, None, :], jnp.stack(log_list))


def solution(mesh):
    return jax.shard_map(
        body,
        mesh=mesh,
        in_specs=(
            P(("dst", "src"), None, None),
            P(("dst", "src")),
            P(("dst", "src")),
            P(None, "dst", "src", None),
            P(None, None, "dst", "src", None),
            P(None, None, "dst", "src", None),
        ),
        out_specs=(P(("dst", "src"), None, None), P(None, "dst", "src", None), P()),
        check_vma=False,
    )
```

profile of v0, /device:TPU:32, one launch (start us, length us, event | category | flops | bytes accessed | tf_op | source)
XLA Modules:
  0.0 727.3 jit_solution(5440016924613923832)
XLA Ops:
  7.2 0.8 compare_and_fusion
  8.1 0.8 fusion.35
  8.9 0.9 fusion.24
  9.7 13.2 %all_gather.13 = bf16[32,4,8,128]{3,0,1,2:T(8,128)(2,1)S(1)} all-gather(bf16[32,4,1,128]{3,0,1,2:T(8,128)(2,1)S(1)} %fusion.24), channel_id=1, replica_groups=mesh['dst'=32,'src'=8] {'src'}, dimensions={2}, use_global_device_ids=true | all-gather | bytes 294912 | tf_op jit(solution)/shard_map/all_gather | solution.py:28
  23.2 1.4 gather_fusion.1
  24.6 2.3 convolution_multiply_fusion.1
  26.9 1.6 broadcast.28.clone
  28.5 8.7 %scatter_fusion = f32[128,32,128]{2,1,0:T(8,128)} fusion(f32[128,32,128]{2,1,0:T(8,128)} %broadcast.28.clone, s32[64]{0:T(128)S(1)} %get-tuple-element.28, f32[64,32,128]{2,1,0:T(8,128)S(1)} %convolution_multiply_fusion.1), kind=kCustom, calls=%fused_computation.6 | custom fusion | flops 262144 | bytes 3145984 | tf_op jit(solution)/shard_map/scatter-add | solution.py:38
  37.3 0.6 copy.54
  38.0 0.6 copy.52
  38.8 219.0 %reduce-scatter.3.cloned.1.call-done = f32[4,32,128]{2,1,0:T(8,128)} async-done(((f32[128,32,128]{2,1,0:T(8,128)}), f32[4,32,128]{2,1,0:T(8,128)}) %reduce-scatter.3.cloned.1.call-update) | async-done | bytes 65552 | tf_op jit(solution)/shard_map/reduce_scatter | solution.py:39
  257.8 1.0 multiply_reduce_fusion.1
  258.7 75.4 %psum.14 = f32[32]{0:T(128)S(1)} all-reduce(f32[32]{0:T(128)S(1)} %multiply_reduce_fusion.1), channel_id=1, replica_groups=mesh['dst'=32,'src'=8] {'dst','src'}, use_global_device_ids=true, to_apply=%region_2.5 | all-reduce | flops 32 | bytes 256 | tf_op jit(solution)/shard_map/psum | solution.py:44
  334.2 0.9 fusion.23
  335.1 11.5 %all-gather.2 = bf16[32,4,1024]{2,0,1:T(8,128)(2,1)S(1)} all-gather(bf16[32,4,128]{2,0,1:T(8,128)(2,1)S(1)} %fusion.23), channel_id=4, replica_groups=mesh['dst'=32,'src'=8] {'src'}, dimensions={2}, use_global_device_ids=true | all-gather | bytes 294912 | tf_op jit(solution)/shard_map/all_gather | solution.py:28
  347.1 0.6 copy-done.1
  347.7 1.4 gather_fusion.4
  349.1 2.3 convolution_multiply_fusion
  351.4 1.6 broadcast.28
  353.0 8.7 %scatter_fusion.1 = f32[128,32,128]{2,1,0:T(8,128)} fusion(f32[128,32,128]{2,1,0:T(8,128)} %broadcast.28, s32[64]{0:T(128)S(1)} %copy-done.6, f32[64,32,128]{2,1,0:T(8,128)S(1)} %convolution_multiply_fusion), kind=kCustom, calls=%fused_computation.7 | custom fusion | flops 262144 | bytes 3145984 | tf_op jit(solution)/shard_map/scatter-add | solution.py:38
  361.8 1.9 gather_fusion.3
  363.7 48.5 %all-gather.6.cloned.1.call-done = bf16[1,32,128,1,128]{4,1,3,0,2:T(8,128)(2,1)} async-done(((bf16[1,32,4,1,128]{4,1,3,0,2:T(8,128)(2,1)}), bf16[1,32,128,1,128]{4,1,3,0,2:T(8,128)(2,1)}) %all-gather.6.cloned.1.call-update) | async-done | bytes 1048592 | tf_op jit(solution)/shard_map/all_gather | solution.py:30
  412.1 2.6 gather_fusion
  414.9 1.4 gather_fusion.2
  416.3 216.4 %reduce-scatter.5.cloned.1.call-done = f32[4,32,128]{2,1,0:T(8,128)} async-done(((f32[128,32,128]{2,1,0:T(8,128)}), f32[4,32,128]{2,1,0:T(8,128)}) %reduce-scatter.5.cloned.1.call-update) | async-done | bytes 65552 | tf_op jit(solution)/shard_map/reduce_scatter | solution.py:39
  632.7 1.0 multiply_reduce_fusion
  633.7 4.1 fusion.3
  637.8 75.1 %psum.15 = f32[32]{0:T(128)S(1)} all-reduce(f32[32]{0:T(128)S(1)} %multiply_reduce_fusion), channel_id=1, replica_groups=mesh['dst'=32,'src'=8] {'dst','src'}, use_global_device_ids=true, to_apply=%region_5.8 | all-reduce | flops 32 | bytes 256 | tf_op jit(solution)/shard_map/psum | solution.py:44
  713.1 0.7 copy.41
  713.8 1.4 gather_fusion.5
  715.2 0.6 pad_maximum_fusion
  715.8 5.0 multiply_convert_fusion
  (36 shorter events, 1.4 us)
Async XLA Ops:
  7.2 17.5 %copy-start = (bf16[64,128,128]{2,1,0:T(8,128)(2,1)S(1)}, bf16[64,128,128]{2,1,0:T(8,128)(2,1)}, u32[]{:S(2)}) copy-start(bf16[64,128,128]{2,1,0:T(8,128)(2,1)} %param.10) | copy-start | bytes 6291460
  7.2 250.6 %reduce-scatter.3.cloned.1.call-start = ((), (), s32[]{:S(2)}) async-start(), calls=%async_computation.2 | async-start | bytes 2162688 | tf_op jit(solution)/shard_map/reduce_scatter | solution.py:39
  8.1 20.5 %copy-start.5 = (s32[64]{0:T(128)}, s32[64]{0:T(128)S(1)}, u32[]{:S(2)}) copy-start(s32[64]{0:T(128)S(1)} %get-tuple-element.28) | copy-start | bytes 772
  28.5 8.8 %copy-start.4 = (bf16[2,32,4,1,128]{4,2,3,1,0:T(4,128)(2,1)S(1)}, bf16[2,32,4,1,128]{4,2,3,1,0:T(4,128)(2,1)}, u32[]{:S(2)}) copy-start(bf16[2,32,4,1,128]{4,2,3,1,0:T(4,128)(2,1)} %param.15) | copy-start | bytes 196612
  37.2 324.5 %all-gather.8.cloned.1.call-start = ((), (), s32[]{:S(2)}) async-start(), calls=%async_computation.5 | async-start | bytes 1081344 | tf_op jit(solution)/shard_map/all_gather | solution.py:30
  38.0 374.1 %all-gather.6.cloned.1.call-start = ((), (), s32[]{:S(2)}) async-start(), calls=%async_computation.4 | async-start | bytes 1081344 | tf_op jit(solution)/shard_map/all_gather | solution.py:30
  38.7 594.0 %reduce-scatter.5.cloned.1.call-start = ((), (), s32[]{:S(2)}) async-start(), calls=%async_computation.3 | async-start | bytes 2162688 | tf_op jit(solution)/shard_map/reduce_scatter | solution.py:39
  347.0 0.7 copy-start.1
  349.1 3.9 copy-start.6
  633.7 79.2 %copy-start.2 = (bf16[32,32,128]{2,1,0:T(8,128)(2,1)S(1)}, bf16[32,32,128]{2,1,0:T(8,128)(2,1)}, u32[]{:S(2)}) copy-start(bf16[32,32,128]{2,1,0:T(8,128)(2,1)} %copy-done.1) | copy-start | bytes 786436
  633.7 79.3 %copy-start.3 = (f32[4,32,128]{2,1,0:T(8,128)S(1)}, f32[4,32,128]{2,1,0:T(8,128)}, u32[]{:S(2)}) copy-start(f32[4,32,128]{2,1,0:T(8,128)} %reduce-scatter.5.cloned.1.call-done) | copy-start | bytes 196612
Sparse Core Ops, SparseCore 0:
  37.4 220.3 reduce-scatter.2
  260.4 74.6 all-gather.7
  338.2 73.8 all-gather.5
  416.4 216.2 reduce-scatter.4
where the time goes:
time: 730 us; the launch traced here: 727 us
  waiting for transfers between devices  484 us (66%)
  blocking collectives  175 us (24%)
  other arithmetic  22.8 us (3%)
  local copies, waits for them, and re-layouts  17.5 us (2%)
  between operations  13.9 us (2%)
  matrix products  13.7 us (2%)
    reduce_scatter x2, waiting for transfers between devices, body(): lax.psum_scatter(partial_value, 'dst', scatter_dimension=0, tiled=True)  435 us
    psum x2, blocking collectives, body(): scale_now = lax.psum(local_term, ('dst', 'src')) / S  151 us
    all_gather x2, waiting for transfers between devices, body(): alpha_rows = lax.all_gather(forward[step_index], 'dst', axis=1, tiled=True)  48.5 us
    all_gather x2, blocking collectives, body(): columns = lax.all_gather(message[:, :, None, :], 'src', axis=2, tiled=True)  24.7 us
    scatter-add x2, other arithmetic, body(): jax.ops.segment_sum(products, row_local, num_segments=total_rows)  17.4 us
  transfers between devices with their start and end apart: 4, of which 3 were waited for; matrix products, arithmetic and copies ran while one was open for 3% of the time, Pallas kernels for 0%

commit v1 on v0

v1 whole, which is shorter than its diff:
```python
import functools

import jax
import jax.numpy as jnp
from jax import lax
from jax.experimental import pallas as pl
from jax.experimental.pallas import tpu as pltpu
from jax.sharding import Mesh
from jax.sharding import PartitionSpec as P

S = 131072
STEPS = 2
NY, NZ, NX, NC = 4, 8, 4, 2
DST = ("y", "z")
SRC = ("x", "c")
ALL = DST + SRC
F32 = jnp.float32
BF16 = jnp.bfloat16
LIMIT = 24 * 1024 * 1024


def vmem(count):
    return [pl.BlockSpec(memory_space=pltpu.VMEM)] * count


def smem(count):
    return [pl.BlockSpec(memory_space=pltpu.SMEM)] * count


def row_of(column, offset):
    b = column.shape[0]
    lane = lax.broadcasted_iota(jnp.int32, (b, 128), 1)
    seq = lax.broadcasted_iota(jnp.int32, (b, 128), 0)
    return jnp.sum(jnp.where(lane == seq + offset, column, 0.0), axis=0, keepdims=True)


def column_of(row, offset, b):
    lane = lax.broadcasted_iota(jnp.int32, (b, 128), 1)
    seq = lax.broadcasted_iota(jnp.int32, (b, 128), 0)
    wide = jnp.broadcast_to(row, (b, 128))
    return jnp.sum(jnp.where(lane == seq + offset, wide, 0.0), axis=1, keepdims=True)


def multiply_slots(index, pieces, blocks, cols, acc):
    rows = pieces[0].shape[0]
    for n, piece in enumerate(pieces):
        cols[n * rows : (n + 1) * rows] = piece[...]
    acc[...] = jnp.zeros_like(acc)
    group = 8

    def several(g, carry):
        for n in range(group):
            m = g * group + n
            product = lax.dot_general(
                cols[index[1, m]],
                blocks[m],
                (((1,), (1,)), ((), ())),
                preferred_element_type=F32,
            )
            row = index[0, m]
            acc[row] = acc[row] + product
        return carry

    lax.fori_loop(0, blocks.shape[0] // group, several, 0)


def first_step(index, *refs):
    pieces, (blocks, out, cols, acc) = refs[:8], refs[8:]
    multiply_slots(index, pieces, blocks, cols, acc)
    total = out.shape[0] * out.shape[1]
    out[...] = acc[:total].astype(BF16).reshape(out.shape)


def second_step(index, place, *refs):
    pieces, forwards, (blocks, first_sum, out, norms, cols, acc) = refs[:8], refs[8:12], refs[12:]
    multiply_slots(index, pieces, blocks, cols, acc)
    total = out.shape[0] * out.shape[1]
    out[...] = acc[:total].astype(BF16).reshape(out.shape)
    b = out.shape[2]
    rows = forwards[0].shape[0]
    y = place[0]
    value = jnp.zeros((b, 128), F32)
    for k, alpha in enumerate(forwards):
        base = lax.rem(y - k + NY, NY) * rows
        for r in range(rows):
            value = value + acc[base + r] * alpha[r, 1].astype(F32)
    part = row_of(jnp.sum(value, axis=1, keepdims=True), b)
    both = part + first_sum[...]
    norms[...] = jnp.broadcast_to(both[None], norms.shape)


def reduce_first(received, emitted, alpha, message, norm):
    total = received[0].astype(F32)
    for d in range(1, received.shape[0]):
        total = total + received[d].astype(F32)
    message[...] = (emitted[...].astype(F32) * total).astype(BF16)
    value = jnp.sum(total * alpha[...].astype(F32), axis=0)
    norm[...] = row_of(jnp.sum(value, axis=1, keepdims=True), 0)


def reduce_last(received, norms, out):
    total = received[0].astype(F32)
    for d in range(1, received.shape[0]):
        total = total + received[d].astype(F32)
    b = total.shape[1]
    norm = jnp.sum(norms[...], axis=0)
    inverse = S / column_of(norm, b, b)
    for a in range(total.shape[0]):
        out[:, a, :] = total[a] * inverse


def count_slots(index, live, *refs):
    pieces, forwards, (norms, blocks, out, logs, weighted, alphas) = refs[:16], refs[16:20], refs[20:]
    rows, b = pieces[0].shape[0], pieces[0].shape[1]

    @pl.when(pl.program_id(0) == 0)
    def _():
        norm = jnp.sum(norms[...], axis=0)
        for k in range(STEPS):
            column = column_of(norm, k * b, b)
            inverse = S / column
            for n in range(8):
                piece = pieces[8 * k + n][...].astype(F32)
                weighted[n * rows : (n + 1) * rows, k] = (piece * inverse).astype(BF16)
        per = forwards[0].shape[0]
        for k, alpha in enumerate(forwards):
            alphas[k * per : (k + 1) * per] = alpha[...]
        lane = lax.broadcasted_iota(jnp.int32, (1, 128), 1)
        first = jnp.where(lane < b, norm, 1.0)
        second = jnp.where((lane >= b) & (lane < 2 * b), norm, 1.0)
        moved = pltpu.roll(second, 128 - b, 1)
        logs[0:1, :] = jnp.log(first / S)
        logs[1:2, :] = jnp.log(moved / first)

    step = pl.program_id(0)
    for n in range(out.shape[0]):
        m = step * out.shape[0] + n
        left = alphas[index[2, m]].reshape(STEPS * b, 128)
        right = weighted[index[1, m]].reshape(STEPS * b, 128)
        total = lax.dot_general(
            left, right, (((0,), (0,)), ((), ())), preferred_element_type=F32
        )
        value = total * blocks[n].astype(F32)
        out[n] = jnp.where(m < live[0], value, 0.0).astype(BF16)


def gather_src(piece):
    found = [piece]
    for k in range(1, NX):
        found.append(lax.ppermute(piece, "x", [(i, (i + k) % NX) for i in range(NX)]))
    out = []
    for item in found:
        out.append(item)
        out.append(lax.ppermute(item, "c", [(0, 1), (1, 0)]))
    return out


def body(transitions, row_block, col_block, beta_last, emissions, forward):
    slots = transitions.shape[0]
    b, rows, width = beta_last.shape[0], beta_last.shape[1], beta_last.shape[3]
    owners = NY * NZ
    src = NX * NC
    total_rows = rows * owners
    y, x, c = lax.axis_index("y"), lax.axis_index("x"), lax.axis_index("c")

    living = row_block >= 0
    row_local = jnp.where(living, row_block // src, 0)
    col_local = jnp.where(living, col_block % (rows * src), 0)
    col_src = col_local % src
    place = ((x - col_src // NC) % NX) * NC + (col_src % NC + c) % NC
    col_index = place * rows + col_local // src
    per = total_rows // NY
    alpha_index = ((y - row_local // per) % NY) * per + row_local % per
    index = jnp.stack([jnp.where(living, row_local, total_rows), col_index, alpha_index])
    live = jnp.sum(living.astype(jnp.int32)).reshape(1)
    y_place = y.astype(jnp.int32).reshape(1)

    emitted = jnp.transpose(emissions[:, :, :, 0, :], (0, 2, 1, 3))
    alpha = jnp.transpose(forward[:, :, :, 0, :], (2, 0, 1, 3))
    beta = jnp.transpose(beta_last[:, :, 0, :], (1, 0, 2))
    message = (emitted[0].astype(F32) * beta).astype(BF16)

    pieces = gather_src(message)

    spread = jnp.broadcast_to(alpha[None], (NZ,) + alpha.shape)
    column = lax.all_to_all(spread, "z", 0, 0)
    column = column.reshape((NZ * rows,) + alpha.shape[1:])
    forwards = [column] + [
        lax.ppermute(column, "y", [(i, (i + k) % NY) for i in range(NY)]) for k in range(1, NY)
    ]

    partial_shape = jax.ShapeDtypeStruct((owners, rows, b, width), BF16)
    slot_scratch = [
        pltpu.VMEM((src * rows, b, width), BF16),
        pltpu.VMEM((total_rows + 8, b, width), F32),
    ]
    params = pltpu.CompilerParams(vmem_limit_bytes=LIMIT)

    sent = pl.pallas_call(
        first_step,
        out_shape=partial_shape,
        in_specs=smem(1) + vmem(9),
        out_specs=vmem(1)[0],
        scratch_shapes=slot_scratch,
        compiler_params=params,
        name="first_step",
    )(index, *pieces, transitions)
    received = lax.all_to_all(sent, DST, 0, 0)

    message_1, norm_0 = pl.pallas_call(
        reduce_first,
        out_shape=(
            jax.ShapeDtypeStruct((rows, b, width), BF16),
            jax.ShapeDtypeStruct((1, 128), F32),
        ),
        in_specs=vmem(3),
        out_specs=tuple(vmem(2)),
        compiler_params=params,
        name="reduce_first",
    )(received, emitted[1], alpha[:, 0])
    pieces_1 = gather_src(message_1)

    sent_1, norms = pl.pallas_call(
        second_step,
        out_shape=(partial_shape, jax.ShapeDtypeStruct((owners * src, 1, 128), F32)),
        in_specs=smem(2) + vmem(14),
        out_specs=tuple(vmem(2)),
        scratch_shapes=slot_scratch,
        compiler_params=params,
        name="second_step",
    )(index, y_place, *pieces_1, *forwards, transitions, norm_0)
    received_1 = lax.all_to_all(sent_1, DST, 0, 0)
    all_norms = lax.all_to_all(norms, ALL, 0, 0)

    group = 8
    whole = lambda shape: pl.BlockSpec(shape, lambda i: (0,) * len(shape))
    part = pl.BlockSpec((group, width, width), lambda i: (i, 0, 0))
    counts, logs = pl.pallas_call(
        count_slots,
        grid=(slots // group,),
        out_shape=(
            jax.ShapeDtypeStruct((slots, width, width), BF16),
            jax.ShapeDtypeStruct((STEPS, 128), F32),
        ),
        in_specs=smem(2)
        + [whole((rows, b, width))] * 16
        + [whole((NZ * rows, STEPS, b, width))] * 4
        + [whole((owners * src, 1, 128)), part],
        out_specs=(part, whole((STEPS, 128))),
        scratch_shapes=[
            pltpu.VMEM((src * rows, STEPS, b, width), BF16),
            pltpu.VMEM((total_rows, STEPS, b, width), BF16),
        ],
        compiler_params=params,
        name="count_slots",
    )(index, live, *pieces, *pieces_1, *forwards, all_norms, transitions)

    beta_first = pl.pallas_call(
        reduce_last,
        out_shape=jax.ShapeDtypeStruct((b, rows, width), F32),
        in_specs=vmem(2),
        out_specs=vmem(1)[0],
        compiler_params=params,
        name="reduce_last",
    )(received_1, all_norms)
    return counts, beta_first[:, :, None, :], logs[:, :b]


def solution(mesh):
    fine = Mesh(mesh.devices.reshape(NY, NZ, NX, NC), ALL)
    return jax.shard_map(
        body,
        mesh=fine,
        in_specs=(
            P(ALL, None, None),
            P(ALL),
            P(ALL),
            P(None, DST, SRC, None),
            P(None, None, DST, SRC, None),
            P(None, None, DST, SRC, None),
        ),
        out_specs=(P(ALL, None, None), P(None, DST, SRC, None), P()),
        check_vma=False,
    )
```

time: 730 us -> 143 us (0.20)
  waiting for transfers between devices: 484 us -> 45.8 us
  blocking collectives: 175 us -> 23.1 us
  starting transfers between devices: 0.16 us -> 40.8 us
  other arithmetic: 22.8 us -> 2.19 us
  Pallas kernels: 0 us -> 17 us
  matrix products: 13.7 us -> 0 us
  between operations: 13.9 us -> 0.83 us
    reduce_scatter x2 -> x0, waiting for transfers between devices: 435 us -> none  [body(): lax.psum_scatter(partial_value, 'dst', scatter_dimension=0, tiled=True)]
    psum x2 -> x0, blocking collectives: 151 us -> none  [body(): scale_now = lax.psum(local_term, ('dst', 'src')) / S]
    all_gather x2 -> x0, waiting for transfers between devices: 48.5 us -> none  [body(): alpha_rows = lax.all_gather(forward[step_index], 'dst', axis=1, tiled=True)]
    all_to_all x0 -> x3, waiting for transfers between devices: none -> 39.4 us  [the longest x1 23.1 us: body(): received = lax.all_to_all(sent, DST, 0, 0)]
    all_gather x2 -> x0, blocking collectives: 24.7 us -> none  [body(): columns = lax.all_gather(message[:, :, None, :], 'src', axis=2, tiled=True)]
    all_to_all x0 -> x3, starting transfers between devices: none -> 24.1 us  [the longest x1 10.2 us: body(): received = lax.all_to_all(sent, DST, 0, 0)]
    all_to_all x0 -> x1, blocking collectives: none -> 23.1 us  [body(): all_norms = lax.all_to_all(norms, ALL, 0, 0)]
    scatter-add x2 -> x0, other arithmetic: 17.4 us -> none  [body(): jax.ops.segment_sum(products, row_local, num_segments=total_rows)]
  transfers between devices with their start and end apart: 4 -> 20, of which waited for: 3 -> 12; matrix products, arithmetic and copies ran while one was open for 3% -> 2% of each run, Pallas kernels for 0% -> 8%
where the time goes in v1:
time: 143 us; the launch traced here: 142 us
  waiting for transfers between devices  45.8 us (32%)
  starting transfers between devices  40.8 us (29%)
  blocking collectives  23.1 us (16%)
  Pallas kernels  17 us (12%)
  local copies, waits for them, and re-layouts  12.3 us (9%)
  other arithmetic  2.19 us (2%)
    all_to_all x1, waiting for transfers between devices, body(): received = lax.all_to_all(sent, DST, 0, 0)  23.1 us
    all_to_all x1, blocking collectives, body(): all_norms = lax.all_to_all(norms, ALL, 0, 0)  23.1 us
    all_to_all x1, waiting for transfers between devices, body(): received_1 = lax.all_to_all(sent_1, DST, 0, 0)  16.3 us
    unnamed x44, local copies, waits for them, and re-layouts  10.5 us
    all_to_all x1, starting transfers between devices, body(): received = lax.all_to_all(sent, DST, 0, 0)  10.2 us
    ppermute x6, starting transfers between devices, gather_src(): lax.ppermute(piece, 'x', [(i, (i + k) % NX) for i in range(NX)])  9.37 us
    all_to_all x1, starting transfers between devices, body(): column = lax.all_to_all(spread, 'z', 0, 0)  8.57 us
    pallas_call x1, Pallas kernels, body(): pl.pallas_call(count_slots, grid=(slots // group,), out_shape=(jax.ShapeD...  6.56 us
  transfers between devices with their start and end apart: 20, of which 12 were waited for; matrix products, arithmetic and copies ran while one was open for 2% of the time, Pallas kernels for 8%

profile of v1, /device:TPU:32, one launch (start us, length us, event | category | flops | bytes accessed | tf_op | source)
XLA Modules:
  0.0 141.9 jit_solution(12138482073382976698)
XLA Ops:
  0.6 0.9 copy.19
  1.5 0.9 broadcast_in_dim.16
  2.4 8.6 %all-to-all-start.1 = ((bf16[8,4,2,32,128]{4,3,2,1,0:T(8,128)(2,1)}), bf16[8,4,2,32,128]{4,3,2,1,0:T(8,128)(2,1)S(1)}, u32[]{:S(2)}, u32[]{:S(2)}) async-start(bf16[8,4,2,32,128]{4,3,2,1,0:T(8,128)(2,1)} %broadcast_in_dim.16), calls=%async_computation.1 | async-start | bytes 1048576 | tf_op jit(solution)/shard_map/all_to_all | solution.py:186
  11.0 0.8 copy.21
  11.8 0.9 fusion.refs_0_
  12.7 1.6 %collective-permute-start.1 = (bf16[4,32,128]{2,1,0:T(8,128)(2,1)S(1)}, bf16[4,32,128]{2,1,0:T(8,128)(2,1)S(1)}, u32[]{:S(2)}, u32[]{:S(2)}) collective-permute-start(bf16[4,32,128]{2,1,0:T(8,128)(2,1)S(1)} %fusion.refs_0_), channel_id=1, source_target_pairs={{0,2},{2,4},{4,6},{6,0},{1,3},{3,5},{5,7},{7,1},{8,10},{10,12},{12... | collective-permute-start | bytes 98312 | tf_op jit(solution)/shard_map/ppermute | solution.py:150
  14.2 2.7 %collective-permute-start.3 = (bf16[4,32,128]{2,1,0:T(8,128)(2,1)S(1)}, bf16[4,32,128]{2,1,0:T(8,128)(2,1)S(1)}, u32[]{:S(2)}, u32[]{:S(2)}) collective-permute-start(bf16[4,32,128]{2,1,0:T(8,128)(2,1)S(1)} %fusion.refs_0_), channel_id=1, source_target_pairs={{0,4},{2,6},{4,0},{6,2},{1,5},{3,7},{5,1},{7,3},{8,12},{10,14},{12... | collective-permute-start | bytes 98312 | tf_op jit(solution)/shard_map/ppermute | solution.py:150
  17.0 1.4 %collective-permute-start.5 = (bf16[4,32,128]{2,1,0:T(8,128)(2,1)S(1)}, bf16[4,32,128]{2,1,0:T(8,128)(2,1)S(1)}, u32[]{:S(2)}, u32[]{:S(2)}) collective-permute-start(bf16[4,32,128]{2,1,0:T(8,128)(2,1)S(1)} %fusion.refs_0_), channel_id=1, source_target_pairs={{0,6},{2,0},{4,2},{6,4},{1,7},{3,1},{5,3},{7,5},{8,14},{10,8},{12,... | collective-permute-start | bytes 98312 | tf_op jit(solution)/shard_map/ppermute | solution.py:150
  18.4 1.3 select_bitcast_fusion
  22.1 1.6 %copy-done = bf16[64,128,128]{2,1,0:T(8,128)(2,1)S(1)} copy-done((bf16[64,128,128]{2,1,0:T(8,128)(2,1)S(1)}, bf16[64,128,128]{2,1,0:T(8,128)(2,1)}, u32[]{:S(2)}) %copy-start) | copy-done | bytes 2097176
  23.7 2.9 %first_step.1 = bf16[32,4,32,128]{3,2,1,0:T(8,128)(2,1)S(1)} custom-call(s32[3,64]{1,0:T(4,128)S(1)} %pad_add_fusion.index, bf16[4,32,128]{2,1,0:T(8,128)(2,1)S(1)} %fusion.refs_0_, bf16[4,32,128]{2,1,0:T(8,128)(2,1)S(1)} %collective-permute-done.refs_1_, bf16[4,32,128]{2,1,0:T(8,128)(2,1)S(1)} %collective-permute-done.1.refs_2_, ...), custom_call_target="tpu_custom_call" | custom-call | tf_op jit(solution)/shard_map/first_step/pallas_call | solution.py:199
  26.6 1.0 copy-done.2
  27.5 10.2 %all-to-all-start = ((bf16[32,4,32,128]{3,2,1,0:T(8,128)(2,1)}), bf16[32,4,32,128]{3,2,1,0:T(8,128)(2,1)}, u32[]{:S(2)}, u32[]{:S(2)}) async-start(bf16[32,4,32,128]{3,2,1,0:T(8,128)(2,1)} %copy-done.2), calls=%async_computation | async-start | bytes 2097152 | tf_op jit(solution)/shard_map/all_to_all | solution.py:208
  37.7 1.5 %collective-permute-start.14 = (bf16[32,2,32,128]{3,2,1,0:T(8,128)(2,1)S(1)}, bf16[32,2,32,128]{3,2,1,0:T(8,128)(2,1)S(1)}, u32[]{:S(2)}, u32[]{:S(2)}) collective-permute-start(bf16[32,2,32,128]{3,2,1,0:T(8,128)(2,1)S(1)} %bitcast.41), channel_id=1, source_target_pairs={{0,64},{64,128},{128,192},{192,0},{1,65},{65,129},{129,193},{193,1... | collective-permute-start | bytes 1572872 | tf_op jit(solution)/shard_map/ppermute | solution.py:189
  39.3 2.7 %collective-permute-start.15 = (bf16[32,2,32,128]{3,2,1,0:T(8,128)(2,1)S(1)}, bf16[32,2,32,128]{3,2,1,0:T(8,128)(2,1)}, u32[]{:S(2)}, u32[]{:S(2)}) collective-permute-start(bf16[32,2,32,128]{3,2,1,0:T(8,128)(2,1)S(1)} %bitcast.42), channel_id=1, source_target_pairs={{0,128},{64,192},{128,0},{192,64},{1,129},{65,193},{129,1},{193,65... | collective-permute-start | bytes 1572872 | tf_op jit(solution)/shard_map/ppermute | solution.py:189
  42.0 1.4 collective-permute-start.16
  43.5 23.1 %all-to-all-done.received = bf16[32,4,32,128]{3,2,1,0:T(8,128)(2,1)} async-done(((bf16[32,4,32,128]{3,2,1,0:T(8,128)(2,1)}), bf16[32,4,32,128]{3,2,1,0:T(8,128)(2,1)}, u32[]{:S(2)}, u32[]{:S(2)}) %all-to-all-start) | async-done | bytes 1048608 | tf_op jit(solution)/shard_map/all_to_all | solution.py:208
  66.6 1.5 %reduce_first.1 = (bf16[4,32,128]{2,1,0:T(8,128)(2,1)S(1)}, f32[1,128]{1,0:T(1,128)S(1)}) custom-call(bf16[32,4,32,128]{3,2,1,0:T(8,128)(2,1)} %all-to-all-done.received, bf16[4,32,128]{2,1,0:T(8,128)(2,1)S(1)} %slice_bitcast_fusion.1.emitted, bf16[4,32,128]{2,1,0:T(8,128)(2,1)S(1)} %slice_bitcast_fusion.alpha), custom_call_target="tpu_custom_call" | custom-call | tf_op jit(solution)/shard_map/reduce_first/pallas_call | solution.py:210
  68.0 1.6 %collective-permute-start.10 = (bf16[4,32,128]{2,1,0:T(8,128)(2,1)S(1)}, bf16[4,32,128]{2,1,0:T(8,128)(2,1)S(1)}, u32[]{:S(2)}, u32[]{:S(2)}) collective-permute-start(bf16[4,32,128]{2,1,0:T(8,128)(2,1)S(1)} %get-tuple-element.9.refs_0_.refs_8_), channel_id=1, source_target_pairs={{0,4},{2,6},{4,0},{6,2},{1,5},{3,7},{5,1},{7,3},{8,12},{10,14},{12... | collective-permute-start | bytes 98312 | tf_op jit(solution)/shard_map/ppermute | solution.py:150
  69.6 1.3 collective-permute-start.12
  71.7 3.6 %collective-permute-done.15.refs_10_.refs_18_ = bf16[32,2,32,128]{3,2,1,0:T(8,128)(2,1)} collective-permute-done((bf16[32,2,32,128]{3,2,1,0:T(8,128)(2,1)S(1)}, bf16[32,2,32,128]{3,2,1,0:T(8,128)(2,1)}, u32[]{:S(2)}, u32[]{:S(2)}) %collective-permute-start.15) | collective-permute-done | bytes 524320 | tf_op jit(solution)/shard_map/ppermute | solution.py:189
  77.3 3.9 %second_step.1 = (bf16[32,4,32,128]{3,2,1,0:T(8,128)(2,1)S(1)}, f32[256,1,128]{2,1,0:T(1,128)S(1)}) custom-call(s32[3,64]{1,0:T(4,128)S(1)} %pad_add_fusion.index, s32[1]{0:T(128)} %bitcast.17.place, bf16[4,32,128]{2,1,0:T(8,128)(2,1)S(1)} %get-tuple-element.9.refs_0_.refs_8_, bf16[4,32,128]{2,1,0:T(8,128)(2,1)S(1)} %collective-permute-done.7.refs_1_.refs_9_, ...), custom_call_target="tpu_custom_call" | custom-call | tf_op jit(solution)/shard_map/second_step/pallas_call | solution.py:223
  81.3 1.0 copy-done.3
  82.3 23.1 %all_to_all.20.refs_20_.norms = f32[256,1,128]{2,1,0:T(1,128)S(1)} all-to-all(f32[256,1,128]{2,1,0:T(1,128)S(1)} %get-tuple-element.11), channel_id=1, replica_groups=mesh['y'=4,'z'=8,'x'=4,'c'=2] {'y','z','x','c'}, dimensions={0} | all-to-all | bytes 262144 | tf_op jit(solution)/shard_map/all_to_all | solution.py:233
  105.3 5.4 %all-to-all-start.3 = ((bf16[32,4,32,128]{3,2,1,0:T(8,128)(2,1)}), bf16[32,4,32,128]{3,2,1,0:T(8,128)(2,1)}, u32[]{:S(2)}, u32[]{:S(2)}) async-start(bf16[32,4,32,128]{3,2,1,0:T(8,128)(2,1)} %copy-done.3), calls=%async_computation.3 | async-start | bytes 2097152 | tf_op jit(solution)/shard_map/all_to_all | solution.py:232
  111.5 0.8 copy-done.7
  112.2 0.8 copy-done.9
  113.0 0.8 copy-done.11
  113.7 0.8 copy-done.13
  116.8 6.6 %count_slots.1 = (bf16[64,128,128]{2,1,0:T(8,128)(2,1)}, f32[2,128]{1,0:T(2,128)}) custom-call(s32[3,64]{1,0:T(4,128)S(1)} %pad_add_fusion.index, s32[1]{0:T(128)} %bitcast.3.live, bf16[4,32,128]{2,1,0:T(8,128)(2,1)S(1)} %fusion.refs_0_, bf16[4,32,128]{2,1,0:T(8,128)(2,1)S(1)} %collective-permute-done.refs_1_, ...), custom_call_target="tpu_custom_call" | custom-call | tf_op jit(solution)/shard_map/count_slots/pallas_call | solution.py:238
  123.3 16.3 %all-to-all-done.3.received = bf16[32,4,32,128]{3,2,1,0:T(8,128)(2,1)} async-done(((bf16[32,4,32,128]{3,2,1,0:T(8,128)(2,1)}), bf16[32,4,32,128]{3,2,1,0:T(8,128)(2,1)}, u32[]{:S(2)}, u32[]{:S(2)}) %all-to-all-start.3) | async-done | bytes 1048608 | tf_op jit(solution)/shard_map/all_to_all | solution.py:232
  139.6 2.3 %reduce_last.1 = f32[32,4,128]{2,1,0:T(4,128)} custom-call(bf16[32,4,32,128]{3,2,1,0:T(8,128)(2,1)} %all-to-all-done.3.received, f32[256,1,128]{2,1,0:T(1,128)S(1)} %all_to_all.20.refs_20_.norms), custom_call_target="tpu_custom_call" | custom-call | tf_op jit(solution)/shard_map/reduce_last/pallas_call | solution.py:258
  (66 shorter events, 8.2 us)
Async XLA Ops:
  2.4 25.1 %all-to-all-start.1 = ((bf16[8,4,2,32,128]{4,3,2,1,0:T(8,128)(2,1)}), bf16[8,4,2,32,128]{4,3,2,1,0:T(8,128)(2,1)S(1)}, u32[]{:S(2)}, u32[]{:S(2)}) async-start(bf16[8,4,2,32,128]{4,3,2,1,0:T(8,128)(2,1)} %broadcast_in_dim.16), calls=%async_computation.1 | async-start | bytes 1048576 | tf_op jit(solution)/shard_map/all_to_all | solution.py:186
  12.7 7.1 %collective-permute-start.1 = (bf16[4,32,128]{2,1,0:T(8,128)(2,1)S(1)}, bf16[4,32,128]{2,1,0:T(8,128)(2,1)S(1)}, u32[]{:S(2)}, u32[]{:S(2)}) collective-permute-start(bf16[4,32,128]{2,1,0:T(8,128)(2,1)S(1)} %fusion.refs_0_), channel_id=1, source_target_pairs={{0,2},{2,4},{4,6},{6,0},{1,3},{3,5},{5,7},{7,1},{8,10},{10,12},{12... | collective-permute-start | bytes 98312 | tf_op jit(solution)/shard_map/ppermute | solution.py:150
  14.2 6.1 %collective-permute-start.3 = (bf16[4,32,128]{2,1,0:T(8,128)(2,1)S(1)}, bf16[4,32,128]{2,1,0:T(8,128)(2,1)S(1)}, u32[]{:S(2)}, u32[]{:S(2)}) collective-permute-start(bf16[4,32,128]{2,1,0:T(8,128)(2,1)S(1)} %fusion.refs_0_), channel_id=1, source_target_pairs={{0,4},{2,6},{4,0},{6,2},{1,5},{3,7},{5,1},{7,3},{8,12},{10,14},{12... | collective-permute-start | bytes 98312 | tf_op jit(solution)/shard_map/ppermute | solution.py:150
  17.0 3.9 %collective-permute-start.5 = (bf16[4,32,128]{2,1,0:T(8,128)(2,1)S(1)}, bf16[4,32,128]{2,1,0:T(8,128)(2,1)S(1)}, u32[]{:S(2)}, u32[]{:S(2)}) collective-permute-start(bf16[4,32,128]{2,1,0:T(8,128)(2,1)S(1)} %fusion.refs_0_), channel_id=1, source_target_pairs={{0,6},{2,0},{4,2},{6,4},{1,7},{3,1},{5,3},{7,5},{8,14},{10,8},{12,... | collective-permute-start | bytes 98312 | tf_op jit(solution)/shard_map/ppermute | solution.py:150
  18.4 2.5 %collective-permute-start = (bf16[4,32,128]{2,1,0:T(8,128)(2,1)S(1)}, bf16[4,32,128]{2,1,0:T(8,128)(2,1)S(1)}, u32[]{:S(2)}, u32[]{:S(2)}) collective-permute-start(bf16[4,32,128]{2,1,0:T(8,128)(2,1)S(1)} %fusion.refs_0_), channel_id=1, source_target_pairs={{0,1},{1,0},{2,3},{3,2},{4,5},{5,4},{6,7},{7,6},{8,9},{9,8},{10,11... | collective-permute-start | bytes 98312 | tf_op jit(solution)/shard_map/ppermute | solution.py:154
  19.7 1.5 %collective-permute-start.2 = (bf16[4,32,128]{2,1,0:T(8,128)(2,1)S(1)}, bf16[4,32,128]{2,1,0:T(8,128)(2,1)S(1)}, u32[]{:S(2)}, u32[]{:S(2)}) collective-permute-start(bf16[4,32,128]{2,1,0:T(8,128)(2,1)S(1)} %collective-permute-done.1.refs_2_), channel_id=1, source_target_pairs={{0,1},{1,0},{2,3},{3,2},{4,5},{5,4},{6,7},{7,6},{8,9},{9,8},{10,11... | collective-permute-start | bytes 98312 | tf_op jit(solution)/shard_map/ppermute | solution.py:154
  20.3 1.2 collective-permute-start.4
  20.9 1.2 collective-permute-start.6
  22.1 1.6 %copy-start = (bf16[64,128,128]{2,1,0:T(8,128)(2,1)S(1)}, bf16[64,128,128]{2,1,0:T(8,128)(2,1)}, u32[]{:S(2)}) copy-start(bf16[64,128,128]{2,1,0:T(8,128)(2,1)} %refs_21_.1) | copy-start | bytes 6291460
  23.7 19.7 %copy-start.20 = (bf16[2,32,4,1,128]{4,2,3,1,0:T(4,128)(2,1)S(1)}, bf16[2,32,4,1,128]{4,2,3,1,0:T(4,128)(2,1)}, u32[]{:S(2)}) copy-start(bf16[2,32,4,1,128]{4,2,3,1,0:T(4,128)(2,1)} %param.11) | copy-start | bytes 196612
  27.5 49.8 %copy-start.1 = (bf16[64,128,128]{2,1,0:T(8,128)(2,1)S(1)}, bf16[64,128,128]{2,1,0:T(8,128)(2,1)}, u32[]{:S(2)}) copy-start(bf16[64,128,128]{2,1,0:T(8,128)(2,1)} %refs_21_.1) | copy-start | bytes 6291460
  27.5 39.0 %all-to-all-start = ((bf16[32,4,32,128]{3,2,1,0:T(8,128)(2,1)}), bf16[32,4,32,128]{3,2,1,0:T(8,128)(2,1)}, u32[]{:S(2)}, u32[]{:S(2)}) async-start(bf16[32,4,32,128]{3,2,1,0:T(8,128)(2,1)} %copy-done.2), calls=%async_computation | async-start | bytes 2097152 | tf_op jit(solution)/shard_map/all_to_all | solution.py:208
  37.7 33.2 %collective-permute-start.14 = (bf16[32,2,32,128]{3,2,1,0:T(8,128)(2,1)S(1)}, bf16[32,2,32,128]{3,2,1,0:T(8,128)(2,1)S(1)}, u32[]{:S(2)}, u32[]{:S(2)}) collective-permute-start(bf16[32,2,32,128]{3,2,1,0:T(8,128)(2,1)S(1)} %bitcast.41), channel_id=1, source_target_pairs={{0,64},{64,128},{128,192},{192,0},{1,65},{65,129},{129,193},{193,1... | collective-permute-start | bytes 1572872 | tf_op jit(solution)/shard_map/ppermute | solution.py:189
  39.3 36.0 %collective-permute-start.15 = (bf16[32,2,32,128]{3,2,1,0:T(8,128)(2,1)S(1)}, bf16[32,2,32,128]{3,2,1,0:T(8,128)(2,1)}, u32[]{:S(2)}, u32[]{:S(2)}) collective-permute-start(bf16[32,2,32,128]{3,2,1,0:T(8,128)(2,1)S(1)} %bitcast.42), channel_id=1, source_target_pairs={{0,128},{64,192},{128,0},{192,64},{1,129},{65,193},{129,1},{193,65... | collective-permute-start | bytes 1572872 | tf_op jit(solution)/shard_map/ppermute | solution.py:189
  42.0 34.3 %collective-permute-start.16 = (bf16[32,2,32,128]{3,2,1,0:T(8,128)(2,1)S(1)}, bf16[32,2,32,128]{3,2,1,0:T(8,128)(2,1)}, u32[]{:S(2)}, u32[]{:S(2)}) collective-permute-start(bf16[32,2,32,128]{3,2,1,0:T(8,128)(2,1)S(1)} %bitcast.43), channel_id=1, source_target_pairs={{0,192},{64,0},{128,64},{192,128},{1,193},{65,1},{129,65},{193,129... | collective-permute-start | bytes 1572872 | tf_op jit(solution)/shard_map/ppermute | solution.py:189
  68.0 13.2 %copy-start.4 = (bf16[4,32,128]{2,1,0:T(8,128)(2,1)}, bf16[4,32,128]{2,1,0:T(8,128)(2,1)S(1)}, u32[]{:S(2)}) copy-start(bf16[4,32,128]{2,1,0:T(8,128)(2,1)S(1)} %get-tuple-element.9.refs_0_.refs_8_) | copy-start | bytes 98308
  68.0 7.3 %collective-permute-start.10 = (bf16[4,32,128]{2,1,0:T(8,128)(2,1)S(1)}, bf16[4,32,128]{2,1,0:T(8,128)(2,1)S(1)}, u32[]{:S(2)}, u32[]{:S(2)}) collective-permute-start(bf16[4,32,128]{2,1,0:T(8,128)(2,1)S(1)} %get-tuple-element.9.refs_0_.refs_8_), channel_id=1, source_target_pairs={{0,4},{2,6},{4,0},{6,2},{1,5},{3,7},{5,1},{7,3},{8,12},{10,14},{12... | collective-permute-start | bytes 98312 | tf_op jit(solution)/shard_map/ppermute | solution.py:150
  69.6 6.2 %collective-permute-start.12 = (bf16[4,32,128]{2,1,0:T(8,128)(2,1)S(1)}, bf16[4,32,128]{2,1,0:T(8,128)(2,1)S(1)}, u32[]{:S(2)}, u32[]{:S(2)}) collective-permute-start(bf16[4,32,128]{2,1,0:T(8,128)(2,1)S(1)} %get-tuple-element.9.refs_0_.refs_8_), channel_id=1, source_target_pairs={{0,6},{2,0},{4,2},{6,4},{1,7},{3,1},{5,3},{7,5},{8,14},{10,8},{12,... | collective-permute-start | bytes 98312 | tf_op jit(solution)/shard_map/ppermute | solution.py:150
  71.0 5.1 %collective-permute-start.8 = (bf16[4,32,128]{2,1,0:T(8,128)(2,1)S(1)}, bf16[4,32,128]{2,1,0:T(8,128)(2,1)S(1)}, u32[]{:S(2)}, u32[]{:S(2)}) collective-permute-start(bf16[4,32,128]{2,1,0:T(8,128)(2,1)S(1)} %get-tuple-element.9.refs_0_.refs_8_), channel_id=1, source_target_pairs={{0,2},{2,4},{4,6},{6,0},{1,3},{3,5},{5,7},{7,1},{8,10},{10,12},{12... | collective-permute-start | bytes 98312 | tf_op jit(solution)/shard_map/ppermute | solution.py:150
  75.3 1.2 collective-permute-start.7
  75.3 5.9 %copy-start.6 = (bf16[4,32,128]{2,1,0:T(8,128)(2,1)}, bf16[4,32,128]{2,1,0:T(8,128)(2,1)S(1)}, u32[]{:S(2)}) copy-start(bf16[4,32,128]{2,1,0:T(8,128)(2,1)S(1)} %collective-permute-done.10.refs_4_.refs_12_) | copy-start | bytes 98308
  75.3 1.4 collective-permute-start.11
  75.8 5.4 %copy-start.8 = (bf16[4,32,128]{2,1,0:T(8,128)(2,1)}, bf16[4,32,128]{2,1,0:T(8,128)(2,1)S(1)}, u32[]{:S(2)}) copy-start(bf16[4,32,128]{2,1,0:T(8,128)(2,1)S(1)} %collective-permute-done.12.refs_6_.refs_14_) | copy-start | bytes 98308
  75.8 1.2 collective-permute-start.13
  76.1 5.1 %copy-start.10 = (bf16[4,32,128]{2,1,0:T(8,128)(2,1)}, bf16[4,32,128]{2,1,0:T(8,128)(2,1)S(1)}, u32[]{:S(2)}) copy-start(bf16[4,32,128]{2,1,0:T(8,128)(2,1)S(1)} %collective-permute-done.8.refs_2_.refs_10_) | copy-start | bytes 98308
  76.1 1.2 collective-permute-start.9
  76.5 4.7 %copy-start.12 = (bf16[4,32,128]{2,1,0:T(8,128)(2,1)}, bf16[4,32,128]{2,1,0:T(8,128)(2,1)S(1)}, u32[]{:S(2)}) copy-start(bf16[4,32,128]{2,1,0:T(8,128)(2,1)S(1)} %collective-permute-done.7.refs_1_.refs_9_) | copy-start | bytes 98308
  76.7 4.6 %copy-start.14 = (bf16[4,32,128]{2,1,0:T(8,128)(2,1)}, bf16[4,32,128]{2,1,0:T(8,128)(2,1)S(1)}, u32[]{:S(2)}) copy-start(bf16[4,32,128]{2,1,0:T(8,128)(2,1)S(1)} %collective-permute-done.11.refs_5_.refs_13_) | copy-start | bytes 98308
  77.0 4.2 %copy-start.16 = (bf16[4,32,128]{2,1,0:T(8,128)(2,1)}, bf16[4,32,128]{2,1,0:T(8,128)(2,1)S(1)}, u32[]{:S(2)}) copy-start(bf16[4,32,128]{2,1,0:T(8,128)(2,1)S(1)} %collective-permute-done.13.refs_7_.refs_15_) | copy-start | bytes 98308
  77.3 4.0 %copy-start.18 = (bf16[4,32,128]{2,1,0:T(8,128)(2,1)}, bf16[4,32,128]{2,1,0:T(8,128)(2,1)S(1)}, u32[]{:S(2)}) copy-start(bf16[4,32,128]{2,1,0:T(8,128)(2,1)S(1)} %collective-permute-done.9.refs_3_.refs_11_) | copy-start | bytes 98308
  81.3 1.0 copy-start.3
  105.3 34.3 %all-to-all-start.3 = ((bf16[32,4,32,128]{3,2,1,0:T(8,128)(2,1)}), bf16[32,4,32,128]{3,2,1,0:T(8,128)(2,1)}, u32[]{:S(2)}, u32[]{:S(2)}) async-start(bf16[32,4,32,128]{3,2,1,0:T(8,128)(2,1)} %copy-done.3), calls=%async_computation.3 | async-start | bytes 2097152 | tf_op jit(solution)/shard_map/all_to_all | solution.py:232
  (9 other events, 7.0 us)

commit v2 on v0

v2 whole, which is shorter than its diff:
```python
import jax
import jax.numpy as jnp
from jax import lax
from jax.experimental import pallas as pl
from jax.experimental.pallas import tpu as pltpu
from jax.sharding import Mesh
from jax.sharding import PartitionSpec as P


S = 131072
STEPS = 2
NY, NH, NL, NX, NC = 4, 4, 2, 4, 2
NZ = NH * NL
SRC_COUNT = NX * NC
DST = ("y", "zh", "zl")
SRC = ("x", "c")
ALL = DST + SRC
F32 = jnp.float32
BF16 = jnp.bfloat16
GRANT = 60 * 1024
EXTRA = 8
CHUNKS = 8
COUNT_GROUP = 16
GROUP = 8


def room(kib):
    return pltpu.CompilerParams(vmem_limit_bytes=(GRANT - kib) * 1024)


def vmem(count):
    return [pl.BlockSpec(memory_space=pltpu.VMEM)] * count


def hbm(count):
    return [pl.BlockSpec(memory_space=pltpu.HBM)] * count


def smem(count):
    return [pl.BlockSpec(memory_space=pltpu.SMEM)] * count


def row_of(column, offset):
    b = column.shape[0]
    lane = lax.broadcasted_iota(jnp.int32, (b, 128), 1)
    seq = lax.broadcasted_iota(jnp.int32, (b, 128), 0)
    return jnp.sum(jnp.where(lane == seq + offset, column, 0.0), axis=0, keepdims=True)


def column_of(row, offset, b):
    lane = lax.broadcasted_iota(jnp.int32, (b, 128), 1)
    seq = lax.broadcasted_iota(jnp.int32, (b, 128), 0)
    wide = jnp.broadcast_to(row, (b, 128))
    return jnp.sum(jnp.where(lane == seq + offset, wide, 0.0), axis=1, keepdims=True)


def tree(values):
    while len(values) > 1:
        values = [values[n] + values[n + 1] for n in range(0, len(values), 2)]
    return values[0]


def over_slots(first, count, step):
    def several(g, carry):
        for n in range(GROUP):
            step(first + g * GROUP + n)
        return carry

    lax.fori_loop(0, count // GROUP, several, 0)


def load_blocks(blocks, held, sems):
    size = held.shape[0] // CHUNKS
    copies = []
    for n in range(CHUNKS):
        part = pl.ds(n * size, size)
        copies.append(pltpu.make_async_copy(blocks.at[part], held.at[part], sems.at[n]))
        copies[-1].start()
    return copies


def over_chunks(copies, held, step):
    size = held.shape[0] // CHUNKS
    for n, copy in enumerate(copies):
        copy.wait()
        over_slots(n * size, size, step)


def split_three(value, rows):
    high = value.astype(BF16).astype(F32)
    middle = (value - high).astype(BF16).astype(F32)
    low = value - high - middle
    line = lax.broadcasted_iota(jnp.int32, (rows, 128), 0)
    return jnp.where(
        line == 0, high, jnp.where(line == 1, middle, jnp.where(line == 2, low, 0.0))
    )


def multiply_slots(index, copies, held, cols, acc):
    acc[...] = jnp.zeros_like(acc)

    def step(m):
        product = lax.dot_general(
            cols[index[1, m]],
            held[m],
            (((1,), (1,)), ((), ())),
            preferred_element_type=F32,
        )
        row = index[0, m]
        acc[row] = acc[row] + product

    over_chunks(copies, held, step)


def send_partials(acc, ready, out, sems, extra=None):
    owners, lines = ready.shape[0], ready.shape[1]
    rows = acc.shape[0] // owners
    kept = rows * acc.shape[1]
    size = owners // CHUNKS
    copies = []
    for n in range(CHUNKS):
        part = pl.ds(n * size, size)
        value = acc[n * size * rows : (n + 1) * size * rows].astype(BF16)
        ready[part, :kept] = value.reshape(size, kept, 128)
        if extra is not None:
            ready[part, kept:] = jnp.broadcast_to(extra[None], (size, lines - kept, 128))
        copies.append(pltpu.make_async_copy(ready.at[part], out.at[part], sems.at[n]))
        copies[-1].start()
    return copies


def first_step(index, *refs):
    pieces, (blocks, out, cols_out) = refs[:SRC_COUNT], refs[SRC_COUNT : SRC_COUNT + 3]
    cols, acc, held, ready, in_sems, out_sems, col_sem = refs[SRC_COUNT + 3 :]
    copies = load_blocks(blocks, held, in_sems)
    rows = pieces[0].shape[0]
    for n, piece in enumerate(pieces):
        cols[n * rows : (n + 1) * rows] = piece[...]
    keep = pltpu.make_async_copy(cols, cols_out, col_sem)
    keep.start()
    multiply_slots(index, copies, held, cols, acc)
    for copy in send_partials(acc, ready, out, out_sems):
        copy.wait()
    keep.wait()


def second_step(index, *refs):
    pieces, (blocks, out, cols_out) = refs[:SRC_COUNT], refs[SRC_COUNT : SRC_COUNT + 3]
    cols, acc, held, ready, in_sems, out_sems, col_sem = refs[SRC_COUNT + 3 :]
    copies = load_blocks(blocks, held, in_sems)
    b = acc.shape[1]
    rows = cols.shape[0] // SRC_COUNT
    parts = []
    for n, piece in enumerate(pieces):
        cols[n * rows : (n + 1) * rows] = piece[: rows * b].reshape(rows, b, 128)
        parts.append(jnp.sum(piece[rows * b :].astype(F32), axis=0, keepdims=True))
    keep = pltpu.make_async_copy(cols, cols_out, col_sem)
    keep.start()
    extra = split_three(tree(parts), EXTRA).astype(BF16)
    multiply_slots(index, copies, held, cols, acc)
    for copy in send_partials(acc, ready, out, out_sems, extra):
        copy.wait()
    keep.wait()


def back_products(index, *refs):
    forwards, (blocks, *outs) = refs[:NY], refs[NY : NY + 1 + SRC_COUNT]
    alphas, acc, held, in_sems, alpha_sems = refs[NY + 1 + SRC_COUNT :]
    per = forwards[0].shape[0]
    loads = []
    for n, alpha in enumerate(forwards):
        part = pl.ds(n * per, per)
        loads.append(pltpu.make_async_copy(alpha, alphas.at[part], alpha_sems.at[n]))
        loads[-1].start()
    copies = load_blocks(blocks, held, in_sems)
    acc[...] = jnp.zeros_like(acc)
    for load in loads:
        load.wait()

    def step(m):
        product = jnp.dot(alphas[index[2, m]], held[m], preferred_element_type=F32)
        col = index[3, m]
        acc[col] = acc[col] + product

    over_chunks(copies, held, step)
    rows = outs[0].shape[0]
    for n, out in enumerate(outs):
        out[...] = acc[n * rows : (n + 1) * rows].astype(BF16)


def add_received(received):
    total = received[0].astype(F32)
    for d in range(1, received.shape[0]):
        total = total + received[d].astype(F32)
    return total


def reduce_first(received, emitted, alpha, *refs):
    backs, message = refs[:SRC_COUNT], refs[SRC_COUNT]
    rows, b = emitted.shape[0], emitted.shape[1]
    total = add_received(received).reshape(rows, b, 128)
    sent = (emitted[...].astype(F32) * total).astype(BF16)
    message[: rows * b] = sent.reshape(rows * b, 128)
    back = tree([piece[...].astype(F32) for piece in backs])
    first = jnp.sum(total * alpha[...].astype(F32), axis=0)
    second = jnp.sum(sent.astype(F32) * back, axis=0)
    norm = row_of(jnp.sum(first, axis=1, keepdims=True), 0)
    norm = norm + row_of(jnp.sum(second, axis=1, keepdims=True), b)
    message[rows * b :] = split_three(norm, EXTRA).astype(BF16)


def norm_of(lines):
    return jnp.sum(jnp.sum(lines.astype(F32), axis=0), axis=0, keepdims=True)


def slot_rows(index, *refs):
    forwards, (out, alphas, sems) = refs[: STEPS * NY], refs[STEPS * NY :]
    per = forwards[0].shape[0]

    @pl.when(pl.program_id(0) == 0)
    def _():
        copies = []
        for k in range(STEPS):
            for n in range(NY):
                at = NY * k + n
                target = alphas.at[pl.ds(n * per, per), k]
                copies.append(pltpu.make_async_copy(forwards[at], target, sems.at[at]))
                copies[-1].start()
        for copy in copies:
            copy.wait()

    step = pl.program_id(0)
    for n in range(out.shape[0]):
        m = step * out.shape[0] + n
        out[n] = alphas[index[2, m]].reshape(out.shape[2], 128).T


def count_slots(index, *refs):
    messages = refs[:STEPS]
    received, left, blocks, out, beta, logs = refs[STEPS : STEPS + 6]
    held, lines, weighted, sems, line_sem = refs[STEPS + 6 :]
    b = weighted.shape[2]
    cols = held.shape[1]

    @pl.when(pl.program_id(0) == 0)
    def _():
        kept = received.shape[1] - EXTRA
        copies = [pltpu.make_async_copy(received, lines, line_sem)]
        for k in range(STEPS):
            copies.append(pltpu.make_async_copy(messages[k], held.at[k], sems.at[k]))
        for copy in copies:
            copy.start()
        for copy in copies:
            copy.wait()
        norm = norm_of(lines[:, kept:])
        weighted[cols] = jnp.zeros((STEPS, b, 128), BF16)
        for k in range(STEPS):
            inverse = S / column_of(norm, k * b, b)
            weighted[:cols, k] = (held[k].astype(F32) * inverse).astype(BF16)
        total = lines[0, :kept].astype(F32)
        for d in range(1, lines.shape[0]):
            total = total + lines[d, :kept].astype(F32)
        inverse = S / column_of(norm, b, b)
        for a in range(kept // b):
            beta[:, a, :] = total[a * b : (a + 1) * b] * inverse
        lane = lax.broadcasted_iota(jnp.int32, (1, 128), 1)
        first = jnp.where(lane < b, norm, 1.0)
        second = jnp.where((lane >= b) & (lane < 2 * b), norm, 1.0)
        moved = pltpu.roll(second, 128 - b, 1)
        logs[0:1, :] = jnp.log(first / S)
        logs[1:2, :] = jnp.log(moved / first)

    step = pl.program_id(0)
    for n in range(out.shape[0]):
        m = step * out.shape[0] + n
        right = weighted[index[3, m]].reshape(STEPS * b, 128)
        total = jnp.dot(left[n], right, preferred_element_type=F32)
        out[n] = (total * blocks[n].astype(F32)).astype(BF16)


def across(value, axis, size, k):
    return lax.ppermute(value, axis, [(i, i ^ k) for i in range(size)])


def gather_src(piece):
    found = [piece] + [across(piece, "x", NX, k) for k in range(1, NX)]
    out = []
    for item in found:
        out.append(item)
        out.append(across(item, "c", NC, 1))
    return out


def gather_y(column):
    return [column] + [across(column, "y", NY, k) for k in range(1, NY)]


def steps(transitions, row_block, col_block, beta_last, emissions, forward):
    slots = transitions.shape[0]
    b, rows, width = beta_last.shape[0], beta_last.shape[1], beta_last.shape[3]
    owners = NY * NZ
    total_rows = rows * owners
    total_cols = rows * SRC_COUNT
    y = lax.axis_index("y")
    mine = lax.axis_index(SRC)

    living = row_block >= 0
    row_local = jnp.where(living, row_block // SRC_COUNT, 0)
    col_local = jnp.where(living, col_block % total_cols, 0)
    col_index = ((col_local % SRC_COUNT) ^ mine) * rows + col_local // SRC_COUNT
    per = total_rows // NY
    alpha_index = ((row_local // per) ^ y) * per + row_local % per
    index = jnp.stack(
        [
            jnp.where(living, row_local, total_rows),
            col_index,
            alpha_index,
            jnp.where(living, col_index, total_cols),
        ]
    )

    emitted = jnp.transpose(emissions[:, :, :, 0, :], (0, 2, 1, 3))
    alpha = jnp.transpose(forward[:, :, :, 0, :], (0, 2, 1, 3))
    beta = jnp.transpose(beta_last[:, :, 0, :], (1, 0, 2))
    message = (emitted[0].astype(F32) * beta).astype(BF16)
    spread = jnp.broadcast_to(alpha[:, None], (STEPS, NZ) + alpha.shape[1:])
    piece_shape = jax.ShapeDtypeStruct((rows, b, width), BF16)

    pieces = gather_src(message)

    columns = lax.all_to_all(spread, ("zh", "zl"), 1, 1)
    columns = columns.reshape(STEPS, NZ * rows, b, width)
    forwards_1 = gather_y(columns[1])
    forwards_0 = gather_y(columns[0])

    def partial_shape(lines):
        return jax.ShapeDtypeStruct((owners, lines, width), BF16)

    def slot_scratch(lines):
        return [
            pltpu.VMEM((total_cols, b, width), BF16),
            pltpu.VMEM((total_rows + 8, b, width), F32),
            pltpu.VMEM((slots, width, width), BF16),
            pltpu.VMEM((owners, lines, width), BF16),
            pltpu.SemaphoreType.DMA((CHUNKS,)),
            pltpu.SemaphoreType.DMA((CHUNKS,)),
            pltpu.SemaphoreType.DMA,
        ]

    lines = rows * b
    cols_shape = jax.ShapeDtypeStruct((total_cols, b, width), BF16)

    sent, cols_0 = pl.pallas_call(
        first_step,
        out_shape=(partial_shape(lines), cols_shape),
        in_specs=smem(1) + vmem(SRC_COUNT) + hbm(1),
        out_specs=tuple(hbm(2)),
        scratch_shapes=slot_scratch(lines),
        compiler_params=room(9000),
        name="first_step",
    )(index, *pieces, transitions)
    received = lax.all_to_all(sent, DST, 0, 0)

    backs = pl.pallas_call(
        back_products,
        out_shape=(piece_shape,) * SRC_COUNT,
        in_specs=smem(1) + hbm(NY + 1),
        out_specs=tuple(vmem(SRC_COUNT)),
        scratch_shapes=[
            pltpu.VMEM((total_rows, b, width), BF16),
            pltpu.VMEM((total_cols + 8, b, width), F32),
            pltpu.VMEM((slots, width, width), BF16),
            pltpu.SemaphoreType.DMA((CHUNKS,)),
            pltpu.SemaphoreType.DMA((NY,)),
        ],
        compiler_params=room(9000),
        name="back_products",
    )(index, *forwards_1, transitions)
    backs = [backs[0]] + [across(backs[n], SRC, SRC_COUNT, n) for n in range(1, SRC_COUNT)]

    message_1 = pl.pallas_call(
        reduce_first,
        out_shape=jax.ShapeDtypeStruct((lines + EXTRA, width), BF16),
        in_specs=vmem(3 + SRC_COUNT),
        out_specs=vmem(1)[0],
        compiler_params=room(9000),
        name="reduce_first",
    )(received, emitted[1], alpha[0], *backs)
    pieces_1 = gather_src(message_1)

    sent_1, cols_1 = pl.pallas_call(
        second_step,
        out_shape=(partial_shape(lines + EXTRA), cols_shape),
        in_specs=smem(1) + vmem(SRC_COUNT) + hbm(1),
        out_specs=tuple(hbm(2)),
        scratch_shapes=slot_scratch(lines + EXTRA),
        compiler_params=room(9000),
        name="second_step",
    )(index, *pieces_1, transitions)
    received_1 = lax.all_to_all(sent_1, DST, 0, 0)

    part = pl.BlockSpec((COUNT_GROUP, width, width), lambda i: (i, 0, 0))
    left_part = pl.BlockSpec((COUNT_GROUP, width, STEPS * b), lambda i: (i, 0, 0))
    left = pl.pallas_call(
        slot_rows,
        grid=(slots // COUNT_GROUP,),
        out_shape=jax.ShapeDtypeStruct((slots, width, STEPS * b), BF16),
        in_specs=smem(1) + hbm(STEPS * NY),
        out_specs=left_part,
        scratch_shapes=[
            pltpu.VMEM((total_rows, STEPS, b, width), BF16),
            pltpu.SemaphoreType.DMA((STEPS * NY,)),
        ],
        compiler_params=room(9000),
        name="slot_rows",
    )(index, *forwards_0, *forwards_1)

    counts, beta_first, logs = pl.pallas_call(
        count_slots,
        grid=(slots // COUNT_GROUP,),
        out_shape=(
            jax.ShapeDtypeStruct((slots, width, width), BF16),
            jax.ShapeDtypeStruct((b, rows, width), F32),
            jax.ShapeDtypeStruct((STEPS, 128), F32),
        ),
        in_specs=smem(1) + hbm(STEPS + 1) + [left_part, part],
        out_specs=(
            part,
            pl.BlockSpec((b, rows, width), lambda i: (0, 0, 0)),
            pl.BlockSpec((STEPS, 128), lambda i: (0, 0)),
        ),
        scratch_shapes=[
            pltpu.VMEM((STEPS, total_cols, b, width), BF16),
            pltpu.VMEM((owners, lines + EXTRA, width), BF16),
            pltpu.VMEM((total_cols + 1, STEPS, b, width), BF16),
            pltpu.SemaphoreType.DMA((STEPS,)),
            pltpu.SemaphoreType.DMA,
        ],
        compiler_params=room(9000),
        name="count_slots",
    )(index, cols_0, cols_1, received_1, left, transitions)
    return counts, beta_first[:, :, None, :], logs[:, :b]


def solution(mesh):
    fine = Mesh(mesh.devices.reshape(NY, NH, NL, NX, NC), ALL)
    return jax.shard_map(
        steps,
        mesh=fine,
        in_specs=(
            P(ALL, None, None),
            P(ALL),
            P(ALL),
            P(None, DST, SRC, None),
            P(None, None, DST, SRC, None),
            P(None, None, DST, SRC, None),
        ),
        out_specs=(P(ALL, None, None), P(None, DST, SRC, None), P()),
        check_vma=False,
    )
```

time: 730 us -> 136 us (0.19)
  waiting for transfers between devices: 484 us -> 54 us
  blocking collectives: 175 us -> 0 us
  starting transfers between devices: 0.16 us -> 55.2 us
  Pallas kernels: 0 us -> 21.4 us
  other arithmetic: 22.8 us -> 1.57 us
  local copies, waits for them, and re-layouts: 17.5 us -> 2.65 us
  matrix products: 13.7 us -> 0 us
  between operations: 13.9 us -> 0.93 us
    reduce_scatter x2 -> x0, waiting for transfers between devices: 435 us -> none  [body(): lax.psum_scatter(partial_value, 'dst', scatter_dimension=0, tiled=True)]
    psum x2 -> x0, blocking collectives: 151 us -> none  [body(): scale_now = lax.psum(local_term, ('dst', 'src')) / S]
    ppermute x0 -> x27, waiting for transfers between devices: none -> 51.8 us  [across(): return lax.ppermute(value, axis, [(i, i ^ k) for i in range(size)])]
    all_gather x2 -> x0, waiting for transfers between devices: 48.5 us -> none  [body(): alpha_rows = lax.all_gather(forward[step_index], 'dst', axis=1, tiled=True)]
    all_to_all x0 -> x3, starting transfers between devices: none -> 29 us  [the longest x1 10.5 us: steps(): received_1 = lax.all_to_all(sent_1, DST, 0, 0)]
    ppermute x0 -> x27, starting transfers between devices: none -> 26.2 us  [across(): return lax.ppermute(value, axis, [(i, i ^ k) for i in range(size)])]
    all_gather x2 -> x0, blocking collectives: 24.7 us -> none  [body(): columns = lax.all_gather(message[:, :, None, :], 'src', axis=2, tiled=True)]
    pallas_call x0 -> x6, Pallas kernels: none -> 21.4 us  [the longest x1 5.3 us: steps(): pl.pallas_call(count_slots, grid=(slots // COUNT_GROUP,), out_shape=(jax....]
  transfers between devices with their start and end apart: 4 -> 30, of which waited for: 3 -> 14; matrix products, arithmetic and copies ran while one was open for 3% -> 2% of each run, Pallas kernels for 0% -> 8%
where the time goes in v2:
time: 136 us
  starting transfers between devices  55.2 us (41%)
  waiting for transfers between devices  54 us (40%)
  Pallas kernels  21.4 us (16%)
  local copies, waits for them, and re-layouts  2.65 us (2%)
  other arithmetic  1.57 us (1%)
    ppermute x27, waiting for transfers between devices, across(): return lax.ppermute(value, axis, [(i, i ^ k) for i in range(size)])  51.8 us
    ppermute x27, starting transfers between devices, across(): return lax.ppermute(value, axis, [(i, i ^ k) for i in range(size)])  26.2 us
    all_to_all x1, starting transfers between devices, steps(): received_1 = lax.all_to_all(sent_1, DST, 0, 0)  10.5 us
    all_to_all x1, starting transfers between devices, steps(): received = lax.all_to_all(sent, DST, 0, 0)  9.99 us
    all_to_all x1, starting transfers between devices, steps(): columns = lax.all_to_all(spread, ('zh', 'zl'), 1, 1)  8.57 us
    pallas_call x1, Pallas kernels, steps(): pl.pallas_call(count_slots, grid=(slots // COUNT_GROUP,), out_shape=(jax....  5.3 us
    pallas_call x1, Pallas kernels, steps(): pl.pallas_call(second_step, out_shape=(partial_shape(lines + EXTRA), cols...  4.73 us
    pallas_call x1, Pallas kernels, steps(): pl.pallas_call(first_step, out_shape=(partial_shape(lines), cols_shape),...  4.7 us
  transfers between devices with their start and end apart: 30, of which 14 were waited for; matrix products, arithmetic and copies ran while one was open for 2% of the time, Pallas kernels for 8%

profile of v2, /device:TPU:32, one launch (start us, length us, event | category | flops | bytes accessed | tf_op | source)
XLA Modules:
  0.0 135.8 jit_solution(6637049552039546761)
XLA Ops:
  0.6 0.9 copy.20
  1.5 0.9 broadcast_in_dim.17
  2.4 8.6 %all-to-all-start.1 = ((bf16[2,8,4,32,128]{4,3,2,0,1:T(8,128)(2,1)}), bf16[2,8,4,32,128]{4,3,2,0,1:T(8,128)(2,1)S(1)}, u32[]{:S(2)}, u32[]{:S(2)}) async-start(bf16[2,8,4,32,128]{4,3,2,0,1:T(8,128)(2,1)} %broadcast_in_dim.17), calls=%async_computation.1 | async-start | bytes 1048576 | tf_op jit(solution)/shard_map/all_to_all | solution.py:331
  11.0 0.8 copy.21
  11.8 0.9 fusion.refs_0_
  12.7 2.8 %collective-permute-start.5 = (bf16[4,32,128]{2,1,0:T(8,128)(2,1)S(1)}, bf16[4,32,128]{2,1,0:T(8,128)(2,1)S(1)}, u32[]{:S(2)}, u32[]{:S(2)}) collective-permute-start(bf16[4,32,128]{2,1,0:T(8,128)(2,1)S(1)} %fusion.refs_0_), channel_id=1, source_target_pairs={{0,6},{2,4},{4,2},{6,0},{1,7},{3,5},{5,3},{7,1},{8,14},{10,12},{12... | collective-permute-start | bytes 98312 | tf_op jit(solution)/shard_map/ppermute | solution.py:282
  15.5 0.8 collective-permute-start.3
  18.2 2.8 %collective-permute-done.3.refs_4_ = bf16[4,32,128]{2,1,0:T(8,128)(2,1)S(1)} collective-permute-done((bf16[4,32,128]{2,1,0:T(8,128)(2,1)S(1)}, bf16[4,32,128]{2,1,0:T(8,128)(2,1)S(1)}, u32[]{:S(2)}, u32[]{:S(2)}) %collective-permute-start.3) | collective-permute-done | bytes 32800 | tf_op jit(solution)/shard_map/ppermute | solution.py:282
  22.3 4.7 %first_step.1 = (bf16[32,128,128]{2,1,0:T(8,128)(2,1)}, bf16[32,32,128]{2,1,0:T(8,128)(2,1)S(1)}) custom-call(s32[4,64]{1,0:T(4,128)S(1)} %pad_add_fusion.index, bf16[4,32,128]{2,1,0:T(8,128)(2,1)S(1)} %fusion.refs_0_, bf16[4,32,128]{2,1,0:T(8,128)(2,1)S(1)} %collective-permute-done.refs_1_, bf16[4,32,128]{2,1,0:T(8,128)(2,1)S(1)} %collective-permute-done.1.refs_2_, ...), custom_call_target="tpu_custom_call" | custom-call | tf_op jit(solution)/shard_map/first_step/pallas_call | solution.py:353
  27.0 10.0 %all-to-all-start = ((bf16[32,128,128]{2,1,0:T(8,128)(2,1)}), bf16[32,128,128]{2,1,0:T(8,128)(2,1)S(1)}, u32[]{:S(2)}, u32[]{:S(2)}) async-start(bf16[32,128,128]{2,1,0:T(8,128)(2,1)} %get-tuple-element.19), calls=%async_computation | async-start | bytes 2097152 | tf_op jit(solution)/shard_map/all_to_all | solution.py:362
  37.1 2.8 %collective-permute-start.9 = (bf16[32,32,128]{2,1,0:T(8,128)(2,1)S(1)}, bf16[32,32,128]{2,1,0:T(8,128)(2,1)S(1)}, u32[]{:S(2)}, u32[]{:S(2)}) collective-permute-start(bf16[32,32,128]{2,1,0:T(8,128)(2,1)S(1)} %bitcast.38), channel_id=1, source_target_pairs={{0,192},{64,128},{128,64},{192,0},{1,193},{65,129},{129,65},{193,1... | collective-permute-start | bytes 786440 | tf_op jit(solution)/shard_map/ppermute | solution.py:282
  39.9 0.8 collective-permute-start.8
  41.3 20.4 %collective-permute-done.9.refs_3_.refs_7_ = bf16[32,32,128]{2,1,0:T(8,128)(2,1)S(1)} collective-permute-done((bf16[32,32,128]{2,1,0:T(8,128)(2,1)S(1)}, bf16[32,32,128]{2,1,0:T(8,128)(2,1)S(1)}, u32[]{:S(2)}, u32[]{:S(2)}) %collective-permute-start.9) | collective-permute-done | bytes 262176 | tf_op jit(solution)/shard_map/ppermute | solution.py:282
  61.6 3.3 %back_products.1 = (bf16[4,32,128]{2,1,0:T(8,128)(2,1)S(1)}, bf16[4,32,128]{2,1,0:T(8,128)(2,1)S(1)}, bf16[4,32,128]{2,1,0:T(8,128)(2,1)S(1)}, bf16[4,32,128]{2,...) custom-call(s32[4,64]{1,0:T(4,128)S(1)} %pad_add_fusion.index, ...), custom_call_target="tpu_custom_call" | custom-call | tf_op jit(solution)/shard_map/back_products/pallas_call | solution.py:364
  65.3 1.5 %collective-permute-start.12 = (bf16[4,32,128]{2,1,0:T(8,128)(2,1)S(1)}, bf16[4,32,128]{2,1,0:T(8,128)(2,1)S(1)}, u32[]{:S(2)}, u32[]{:S(2)}) collective-permute-start(bf16[4,32,128]{2,1,0:T(8,128)(2,1)S(1)} %get-tuple-element.23), channel_id=1, source_target_pairs={{0,3},{1,2},{2,1},{3,0},{4,7},{5,6},{6,5},{7,4},{8,11},{9,10},{10,... | collective-permute-start | bytes 98312 | tf_op jit(solution)/shard_map/ppermute | solution.py:282
  66.9 1.6 %collective-permute-start.13 = (bf16[4,32,128]{2,1,0:T(8,128)(2,1)S(1)}, bf16[4,32,128]{2,1,0:T(8,128)(2,1)S(1)}, u32[]{:S(2)}, u32[]{:S(2)}) collective-permute-start(bf16[4,32,128]{2,1,0:T(8,128)(2,1)S(1)} %get-tuple-element.24), channel_id=1, source_target_pairs={{0,4},{1,5},{2,6},{3,7},{4,0},{5,1},{6,2},{7,3},{8,12},{9,13},{10,... | collective-permute-start | bytes 98312 | tf_op jit(solution)/shard_map/ppermute | solution.py:282
  68.5 1.6 %collective-permute-start.14 = (bf16[4,32,128]{2,1,0:T(8,128)(2,1)S(1)}, bf16[4,32,128]{2,1,0:T(8,128)(2,1)S(1)}, u32[]{:S(2)}, u32[]{:S(2)}) collective-permute-start(bf16[4,32,128]{2,1,0:T(8,128)(2,1)S(1)} %get-tuple-element.25), channel_id=1, source_target_pairs={{0,5},{1,4},{2,7},{3,6},{4,1},{5,0},{6,3},{7,2},{8,13},{9,12},{10,... | collective-permute-start | bytes 98312 | tf_op jit(solution)/shard_map/ppermute | solution.py:282
  70.1 1.0 collective-permute-start.15
  71.1 2.0 %collective-permute-start.16 = (bf16[4,32,128]{2,1,0:T(8,128)(2,1)S(1)}, bf16[4,32,128]{2,1,0:T(8,128)(2,1)S(1)}, u32[]{:S(2)}, u32[]{:S(2)}) collective-permute-start(bf16[4,32,128]{2,1,0:T(8,128)(2,1)S(1)} %get-tuple-element.27), channel_id=1, source_target_pairs={{0,7},{1,6},{2,5},{3,4},{4,3},{5,2},{6,1},{7,0},{8,15},{9,14},{10,... | collective-permute-start | bytes 98312 | tf_op jit(solution)/shard_map/ppermute | solution.py:282
  73.4 1.9 %collective-permute-done.15.refs_6_ = bf16[4,32,128]{2,1,0:T(8,128)(2,1)S(1)} collective-permute-done((bf16[4,32,128]{2,1,0:T(8,128)(2,1)S(1)}, bf16[4,32,128]{2,1,0:T(8,128)(2,1)S(1)}, u32[]{:S(2)}, u32[]{:S(2)}) %collective-permute-start.15) | collective-permute-done | bytes 32800 | tf_op jit(solution)/shard_map/ppermute | solution.py:282
  75.9 2.4 %collective-permute-start.22 = (bf16[136,128]{1,0:T(8,128)(2,1)S(1)}, bf16[136,128]{1,0:T(8,128)(2,1)S(1)}, u32[]{:S(2)}, u32[]{:S(2)}) collective-permute-start(bf16[136,128]{1,0:T(8,128)(2,1)S(1)} %reduce_first.1.refs_0_), channel_id=1, source_target_pairs={{0,6},{2,4},{4,2},{6,0},{1,7},{3,5},{5,3},{7,1},{8,14},{10,12},{12... | collective-permute-start | bytes 104456 | tf_op jit(solution)/shard_map/ppermute | solution.py:282
  78.3 1.8 %collective-permute-start.18 = (bf16[136,128]{1,0:T(8,128)(2,1)S(1)}, bf16[136,128]{1,0:T(8,128)(2,1)S(1)}, u32[]{:S(2)}, u32[]{:S(2)}) collective-permute-start(bf16[136,128]{1,0:T(8,128)(2,1)S(1)} %reduce_first.1.refs_0_), channel_id=1, source_target_pairs={{0,2},{2,0},{4,6},{6,4},{1,3},{3,1},{5,7},{7,5},{8,10},{10,8},{12,... | collective-permute-start | bytes 104456 | tf_op jit(solution)/shard_map/ppermute | solution.py:282
  80.1 1.0 collective-permute-done.22.refs_6_
  81.2 2.6 %collective-permute-done.20.refs_4_ = bf16[136,128]{1,0:T(8,128)(2,1)S(1)} collective-permute-done((bf16[136,128]{1,0:T(8,128)(2,1)S(1)}, bf16[136,128]{1,0:T(8,128)(2,1)S(1)}, u32[]{:S(2)}, u32[]{:S(2)}) %collective-permute-start.20) | collective-permute-done | bytes 34848 | tf_op jit(solution)/shard_map/ppermute | solution.py:282
  85.1 4.7 %second_step.1 = (bf16[32,136,128]{2,1,0:T(8,128)(2,1)}, bf16[32,32,128]{2,1,0:T(8,128)(2,1)S(1)}) custom-call(s32[4,64]{1,0:T(4,128)S(1)} %pad_add_fusion.index, bf16[136,128]{1,0:T(8,128)(2,1)S(1)} %reduce_first.1.refs_0_, bf16[136,128]{1,0:T(8,128)(2,1)S(1)} %collective-permute-done.17.refs_1_, bf16[136,128]{1,0:T(8,128)(2,1)S(1)} %collective-permute-done.18.refs_2_, ...), custom_call_target="tpu_custom_call" | custom-call | tf_op jit(solution)/shard_map/second_step/pallas_call | solution.py:391
  89.9 10.5 %all-to-all-start.2 = ((bf16[32,136,128]{2,1,0:T(8,128)(2,1)}), bf16[32,136,128]{2,1,0:T(8,128)(2,1)S(1)}, u32[]{:S(2)}, u32[]{:S(2)}) async-start(bf16[32,136,128]{2,1,0:T(8,128)(2,1)} %get-tuple-element.29), calls=%async_computation.2 | async-start | bytes 2228224 | tf_op jit(solution)/shard_map/all_to_all | solution.py:400
  100.3 2.8 %collective-permute-start.26 = (bf16[32,32,128]{2,1,0:T(8,128)(2,1)S(1)}, bf16[32,32,128]{2,1,0:T(8,128)(2,1)S(1)}, u32[]{:S(2)}, u32[]{:S(2)}) collective-permute-start(bf16[32,32,128]{2,1,0:T(8,128)(2,1)S(1)} %bitcast.43), channel_id=1, source_target_pairs={{0,192},{64,128},{128,64},{192,0},{1,193},{65,129},{129,65},{193,1... | collective-permute-start | bytes 786440 | tf_op jit(solution)/shard_map/ppermute | solution.py:282
  103.2 0.8 collective-permute-start.25
  104.5 20.5 %collective-permute-done.26.refs_3_ = bf16[32,32,128]{2,1,0:T(8,128)(2,1)S(1)} collective-permute-done((bf16[32,32,128]{2,1,0:T(8,128)(2,1)S(1)}, bf16[32,32,128]{2,1,0:T(8,128)(2,1)S(1)}, u32[]{:S(2)}, u32[]{:S(2)}) %collective-permute-start.26) | collective-permute-done | bytes 262176 | tf_op jit(solution)/shard_map/ppermute | solution.py:282
  125.0 3.1 %slot_rows.1.refs_3_ = bf16[64,128,64]{2,1,0:T(8,128)(2,1)} custom-call(s32[4,64]{1,0:T(4,128)S(1)} %pad_add_fusion.index, bf16[32,32,128]{2,1,0:T(8,128)(2,1)S(1)} %bitcast.46, bf16[32,32,128]{2,1,0:T(8,128)(2,1)S(1)} %collective-permute-done.24.refs_1_, bf16[32,32,128]{2,1,0:T(8,128)(2,1)S(1)} %collective-permute-done.25.refs_2_, ...), custom_call_target="tpu_custom_call" | custom-call | tf_op jit(solution)/shard_map/slot_rows/pallas_call | solution.py:404
  128.1 2.2 %all-to-all-done.2.refs_2_ = bf16[32,136,128]{2,1,0:T(8,128)(2,1)S(1)} async-done(((bf16[32,136,128]{2,1,0:T(8,128)(2,1)}), bf16[32,136,128]{2,1,0:T(8,128)(2,1)S(1)}, u32[]{:S(2)}, u32[]{:S(2)}) %all-to-all-start.2) | async-done | bytes 1114144 | tf_op jit(solution)/shard_map/all_to_all | solution.py:400
  130.3 5.3 %count_slots.1 = (bf16[64,128,128]{2,1,0:T(8,128)(2,1)}, f32[32,4,128]{2,1,0:T(4,128)}, f32[2,128]{1,0:T(2,128)}) custom-call(s32[4,64]{1,0:T(4,128)S(1)} %pad_add_fusion.index, bf16[32,32,128]{2,1,0:T(8,128)(2,1)S(1)} %get-tuple-element.18.refs_0_, bf16[32,32,128]{2,1,0:T(8,128)(2,1)S(1)} %get-tuple-element.28.refs_1_, ...), custom_call_target="tpu_custom_call" | custom-call | tf_op jit(solution)/shard_map/count_slots/pallas_call | solution.py:418
  (44 shorter events, 7.2 us)
Async XLA Ops:
  2.4 24.6 %all-to-all-start.1 = ((bf16[2,8,4,32,128]{4,3,2,0,1:T(8,128)(2,1)}), bf16[2,8,4,32,128]{4,3,2,0,1:T(8,128)(2,1)S(1)}, u32[]{:S(2)}, u32[]{:S(2)}) async-start(bf16[2,8,4,32,128]{4,3,2,0,1:T(8,128)(2,1)} %broadcast_in_dim.17), calls=%async_computation.1 | async-start | bytes 1048576 | tf_op jit(solution)/shard_map/all_to_all | solution.py:331
  12.7 5.2 %collective-permute-start.5 = (bf16[4,32,128]{2,1,0:T(8,128)(2,1)S(1)}, bf16[4,32,128]{2,1,0:T(8,128)(2,1)S(1)}, u32[]{:S(2)}, u32[]{:S(2)}) collective-permute-start(bf16[4,32,128]{2,1,0:T(8,128)(2,1)S(1)} %fusion.refs_0_), channel_id=1, source_target_pairs={{0,6},{2,4},{4,2},{6,0},{1,7},{3,5},{5,3},{7,1},{8,14},{10,12},{12... | collective-permute-start | bytes 98312 | tf_op jit(solution)/shard_map/ppermute | solution.py:282
  15.5 5.4 %collective-permute-start.3 = (bf16[4,32,128]{2,1,0:T(8,128)(2,1)S(1)}, bf16[4,32,128]{2,1,0:T(8,128)(2,1)S(1)}, u32[]{:S(2)}, u32[]{:S(2)}) collective-permute-start(bf16[4,32,128]{2,1,0:T(8,128)(2,1)S(1)} %fusion.refs_0_), channel_id=1, source_target_pairs={{0,4},{2,6},{4,0},{6,2},{1,5},{3,7},{5,1},{7,3},{8,12},{10,14},{12... | collective-permute-start | bytes 98312 | tf_op jit(solution)/shard_map/ppermute | solution.py:282
  16.3 4.6 %collective-permute-start.1 = (bf16[4,32,128]{2,1,0:T(8,128)(2,1)S(1)}, bf16[4,32,128]{2,1,0:T(8,128)(2,1)S(1)}, u32[]{:S(2)}, u32[]{:S(2)}) collective-permute-start(bf16[4,32,128]{2,1,0:T(8,128)(2,1)S(1)} %fusion.refs_0_), channel_id=1, source_target_pairs={{0,2},{2,0},{4,6},{6,4},{1,3},{3,1},{5,7},{7,5},{8,10},{10,8},{12,... | collective-permute-start | bytes 98312 | tf_op jit(solution)/shard_map/ppermute | solution.py:282
  16.8 4.6 %collective-permute-start = (bf16[4,32,128]{2,1,0:T(8,128)(2,1)S(1)}, bf16[4,32,128]{2,1,0:T(8,128)(2,1)S(1)}, u32[]{:S(2)}, u32[]{:S(2)}) collective-permute-start(bf16[4,32,128]{2,1,0:T(8,128)(2,1)S(1)} %fusion.refs_0_), channel_id=1, source_target_pairs={{0,1},{1,0},{2,3},{3,2},{4,5},{5,4},{6,7},{7,6},{8,9},{9,8},{10,11... | collective-permute-start | bytes 98312 | tf_op jit(solution)/shard_map/ppermute | solution.py:282
  17.9 3.6 %collective-permute-start.6 = (bf16[4,32,128]{2,1,0:T(8,128)(2,1)S(1)}, bf16[4,32,128]{2,1,0:T(8,128)(2,1)S(1)}, u32[]{:S(2)}, u32[]{:S(2)}) collective-permute-start(bf16[4,32,128]{2,1,0:T(8,128)(2,1)S(1)} %collective-permute-done.5.refs_6_), channel_id=1, source_target_pairs={{0,1},{1,0},{2,3},{3,2},{4,5},{5,4},{6,7},{7,6},{8,9},{9,8},{10,11... | collective-permute-start | bytes 98312 | tf_op jit(solution)/shard_map/ppermute | solution.py:282
  20.9 1.2 collective-permute-start.4
  20.9 1.4 %collective-permute-start.2 = (bf16[4,32,128]{2,1,0:T(8,128)(2,1)S(1)}, bf16[4,32,128]{2,1,0:T(8,128)(2,1)S(1)}, u32[]{:S(2)}, u32[]{:S(2)}) collective-permute-start(bf16[4,32,128]{2,1,0:T(8,128)(2,1)S(1)} %collective-permute-done.1.refs_2_), channel_id=1, source_target_pairs={{0,1},{1,0},{2,3},{3,2},{4,5},{5,4},{6,7},{7,6},{8,9},{9,8},{10,11... | collective-permute-start | bytes 98312 | tf_op jit(solution)/shard_map/ppermute | solution.py:282
  27.0 48.6 %all-to-all-start = ((bf16[32,128,128]{2,1,0:T(8,128)(2,1)}), bf16[32,128,128]{2,1,0:T(8,128)(2,1)S(1)}, u32[]{:S(2)}, u32[]{:S(2)}) async-start(bf16[32,128,128]{2,1,0:T(8,128)(2,1)} %get-tuple-element.19), calls=%async_computation | async-start | bytes 2097152 | tf_op jit(solution)/shard_map/all_to_all | solution.py:362
  37.1 24.6 %collective-permute-start.9 = (bf16[32,32,128]{2,1,0:T(8,128)(2,1)S(1)}, bf16[32,32,128]{2,1,0:T(8,128)(2,1)S(1)}, u32[]{:S(2)}, u32[]{:S(2)}) collective-permute-start(bf16[32,32,128]{2,1,0:T(8,128)(2,1)S(1)} %bitcast.38), channel_id=1, source_target_pairs={{0,192},{64,128},{128,64},{192,0},{1,193},{65,129},{129,65},{193,1... | collective-permute-start | bytes 786440 | tf_op jit(solution)/shard_map/ppermute | solution.py:282
  39.9 21.8 %collective-permute-start.8 = (bf16[32,32,128]{2,1,0:T(8,128)(2,1)S(1)}, bf16[32,32,128]{2,1,0:T(8,128)(2,1)S(1)}, u32[]{:S(2)}, u32[]{:S(2)}) collective-permute-start(bf16[32,32,128]{2,1,0:T(8,128)(2,1)S(1)} %bitcast.39), channel_id=1, source_target_pairs={{0,128},{64,192},{128,0},{192,64},{1,129},{65,193},{129,1},{193,65... | collective-permute-start | bytes 786440 | tf_op jit(solution)/shard_map/ppermute | solution.py:282
  40.7 20.9 %collective-permute-start.7 = (bf16[32,32,128]{2,1,0:T(8,128)(2,1)S(1)}, bf16[32,32,128]{2,1,0:T(8,128)(2,1)S(1)}, u32[]{:S(2)}, u32[]{:S(2)}) collective-permute-start(bf16[32,32,128]{2,1,0:T(8,128)(2,1)S(1)} %bitcast.40), channel_id=1, source_target_pairs={{0,64},{64,0},{128,192},{192,128},{1,65},{65,1},{129,193},{193,129... | collective-permute-start | bytes 786440 | tf_op jit(solution)/shard_map/ppermute | solution.py:282
  64.9 5.2 %collective-permute-start.10 = (bf16[4,32,128]{2,1,0:T(8,128)(2,1)S(1)}, bf16[4,32,128]{2,1,0:T(8,128)(2,1)S(1)}, u32[]{:S(2)}, u32[]{:S(2)}) collective-permute-start(bf16[4,32,128]{2,1,0:T(8,128)(2,1)S(1)} %get-tuple-element.21), channel_id=1, source_target_pairs={{0,1},{1,0},{2,3},{3,2},{4,5},{5,4},{6,7},{7,6},{8,9},{9,8},{10,11... | collective-permute-start | bytes 98312 | tf_op jit(solution)/shard_map/ppermute | solution.py:282
  65.0 6.1 %collective-permute-start.11 = (bf16[4,32,128]{2,1,0:T(8,128)(2,1)S(1)}, bf16[4,32,128]{2,1,0:T(8,128)(2,1)S(1)}, u32[]{:S(2)}, u32[]{:S(2)}) collective-permute-start(bf16[4,32,128]{2,1,0:T(8,128)(2,1)S(1)} %get-tuple-element.22), channel_id=1, source_target_pairs={{0,2},{1,3},{2,0},{3,1},{4,6},{5,7},{6,4},{7,5},{8,10},{9,11},{10,... | collective-permute-start | bytes 98312 | tf_op jit(solution)/shard_map/ppermute | solution.py:282
  65.3 7.8 %collective-permute-start.12 = (bf16[4,32,128]{2,1,0:T(8,128)(2,1)S(1)}, bf16[4,32,128]{2,1,0:T(8,128)(2,1)S(1)}, u32[]{:S(2)}, u32[]{:S(2)}) collective-permute-start(bf16[4,32,128]{2,1,0:T(8,128)(2,1)S(1)} %get-tuple-element.23), channel_id=1, source_target_pairs={{0,3},{1,2},{2,1},{3,0},{4,7},{5,6},{6,5},{7,4},{8,11},{9,10},{10,... | collective-permute-start | bytes 98312 | tf_op jit(solution)/shard_map/ppermute | solution.py:282
  66.9 6.2 %collective-permute-start.13 = (bf16[4,32,128]{2,1,0:T(8,128)(2,1)S(1)}, bf16[4,32,128]{2,1,0:T(8,128)(2,1)S(1)}, u32[]{:S(2)}, u32[]{:S(2)}) collective-permute-start(bf16[4,32,128]{2,1,0:T(8,128)(2,1)S(1)} %get-tuple-element.24), channel_id=1, source_target_pairs={{0,4},{1,5},{2,6},{3,7},{4,0},{5,1},{6,2},{7,3},{8,12},{9,13},{10,... | collective-permute-start | bytes 98312 | tf_op jit(solution)/shard_map/ppermute | solution.py:282
  68.5 4.9 %collective-permute-start.14 = (bf16[4,32,128]{2,1,0:T(8,128)(2,1)S(1)}, bf16[4,32,128]{2,1,0:T(8,128)(2,1)S(1)}, u32[]{:S(2)}, u32[]{:S(2)}) collective-permute-start(bf16[4,32,128]{2,1,0:T(8,128)(2,1)S(1)} %get-tuple-element.25), channel_id=1, source_target_pairs={{0,5},{1,4},{2,7},{3,6},{4,1},{5,0},{6,3},{7,2},{8,13},{9,12},{10,... | collective-permute-start | bytes 98312 | tf_op jit(solution)/shard_map/ppermute | solution.py:282
  70.1 5.1 %collective-permute-start.15 = (bf16[4,32,128]{2,1,0:T(8,128)(2,1)S(1)}, bf16[4,32,128]{2,1,0:T(8,128)(2,1)S(1)}, u32[]{:S(2)}, u32[]{:S(2)}) collective-permute-start(bf16[4,32,128]{2,1,0:T(8,128)(2,1)S(1)} %get-tuple-element.26), channel_id=1, source_target_pairs={{0,6},{1,7},{2,4},{3,5},{4,2},{5,3},{6,0},{7,1},{8,14},{9,15},{10,... | collective-permute-start | bytes 98312 | tf_op jit(solution)/shard_map/ppermute | solution.py:282
  71.1 4.6 %collective-permute-start.16 = (bf16[4,32,128]{2,1,0:T(8,128)(2,1)S(1)}, bf16[4,32,128]{2,1,0:T(8,128)(2,1)S(1)}, u32[]{:S(2)}, u32[]{:S(2)}) collective-permute-start(bf16[4,32,128]{2,1,0:T(8,128)(2,1)S(1)} %get-tuple-element.27), channel_id=1, source_target_pairs={{0,7},{1,6},{2,5},{3,4},{4,3},{5,2},{6,1},{7,0},{8,15},{9,14},{10,... | collective-permute-start | bytes 98312 | tf_op jit(solution)/shard_map/ppermute | solution.py:282
  75.9 5.2 %collective-permute-start.22 = (bf16[136,128]{1,0:T(8,128)(2,1)S(1)}, bf16[136,128]{1,0:T(8,128)(2,1)S(1)}, u32[]{:S(2)}, u32[]{:S(2)}) collective-permute-start(bf16[136,128]{1,0:T(8,128)(2,1)S(1)} %reduce_first.1.refs_0_), channel_id=1, source_target_pairs={{0,6},{2,4},{4,2},{6,0},{1,7},{3,5},{5,3},{7,1},{8,14},{10,12},{12... | collective-permute-start | bytes 104456 | tf_op jit(solution)/shard_map/ppermute | solution.py:282
  78.3 5.4 %collective-permute-start.20 = (bf16[136,128]{1,0:T(8,128)(2,1)S(1)}, bf16[136,128]{1,0:T(8,128)(2,1)S(1)}, u32[]{:S(2)}, u32[]{:S(2)}) collective-permute-start(bf16[136,128]{1,0:T(8,128)(2,1)S(1)} %reduce_first.1.refs_0_), channel_id=1, source_target_pairs={{0,4},{2,6},{4,0},{6,2},{1,5},{3,7},{5,1},{7,3},{8,12},{10,14},{12... | collective-permute-start | bytes 104456 | tf_op jit(solution)/shard_map/ppermute | solution.py:282
  78.3 5.4 %collective-permute-start.18 = (bf16[136,128]{1,0:T(8,128)(2,1)S(1)}, bf16[136,128]{1,0:T(8,128)(2,1)S(1)}, u32[]{:S(2)}, u32[]{:S(2)}) collective-permute-start(bf16[136,128]{1,0:T(8,128)(2,1)S(1)} %reduce_first.1.refs_0_), channel_id=1, source_target_pairs={{0,2},{2,0},{4,6},{6,4},{1,3},{3,1},{5,7},{7,5},{8,10},{10,8},{12,... | collective-permute-start | bytes 104456 | tf_op jit(solution)/shard_map/ppermute | solution.py:282
  80.1 4.1 %collective-permute-start.17 = (bf16[136,128]{1,0:T(8,128)(2,1)S(1)}, bf16[136,128]{1,0:T(8,128)(2,1)S(1)}, u32[]{:S(2)}, u32[]{:S(2)}) collective-permute-start(bf16[136,128]{1,0:T(8,128)(2,1)S(1)} %reduce_first.1.refs_0_), channel_id=1, source_target_pairs={{0,1},{1,0},{2,3},{3,2},{4,5},{5,4},{6,7},{7,6},{8,9},{9,8},{10,11... | collective-permute-start | bytes 104456 | tf_op jit(solution)/shard_map/ppermute | solution.py:282
  81.2 3.1 %collective-permute-start.23 = (bf16[136,128]{1,0:T(8,128)(2,1)S(1)}, bf16[136,128]{1,0:T(8,128)(2,1)S(1)}, u32[]{:S(2)}, u32[]{:S(2)}) collective-permute-start(bf16[136,128]{1,0:T(8,128)(2,1)S(1)} %collective-permute-done.22.refs_6_), channel_id=1, source_target_pairs={{0,1},{1,0},{2,3},{3,2},{4,5},{5,4},{6,7},{7,6},{8,9},{9,8},{10,11... | collective-permute-start | bytes 104456 | tf_op jit(solution)/shard_map/ppermute | solution.py:282
  83.7 1.2 collective-permute-start.21
  83.7 1.4 %collective-permute-start.19 = (bf16[136,128]{1,0:T(8,128)(2,1)S(1)}, bf16[136,128]{1,0:T(8,128)(2,1)S(1)}, u32[]{:S(2)}, u32[]{:S(2)}) collective-permute-start(bf16[136,128]{1,0:T(8,128)(2,1)S(1)} %collective-permute-done.18.refs_2_), channel_id=1, source_target_pairs={{0,1},{1,0},{2,3},{3,2},{4,5},{5,4},{6,7},{7,6},{8,9},{9,8},{10,11... | collective-permute-start | bytes 104456 | tf_op jit(solution)/shard_map/ppermute | solution.py:282
  89.9 40.5 %all-to-all-start.2 = ((bf16[32,136,128]{2,1,0:T(8,128)(2,1)}), bf16[32,136,128]{2,1,0:T(8,128)(2,1)S(1)}, u32[]{:S(2)}, u32[]{:S(2)}) async-start(bf16[32,136,128]{2,1,0:T(8,128)(2,1)} %get-tuple-element.29), calls=%async_computation.2 | async-start | bytes 2228224 | tf_op jit(solution)/shard_map/all_to_all | solution.py:400
  100.3 24.7 %collective-permute-start.26 = (bf16[32,32,128]{2,1,0:T(8,128)(2,1)S(1)}, bf16[32,32,128]{2,1,0:T(8,128)(2,1)S(1)}, u32[]{:S(2)}, u32[]{:S(2)}) collective-permute-start(bf16[32,32,128]{2,1,0:T(8,128)(2,1)S(1)} %bitcast.43), channel_id=1, source_target_pairs={{0,192},{64,128},{128,64},{192,0},{1,193},{65,129},{129,65},{193,1... | collective-permute-start | bytes 786440 | tf_op jit(solution)/shard_map/ppermute | solution.py:282
  103.2 21.8 %collective-permute-start.25 = (bf16[32,32,128]{2,1,0:T(8,128)(2,1)S(1)}, bf16[32,32,128]{2,1,0:T(8,128)(2,1)S(1)}, u32[]{:S(2)}, u32[]{:S(2)}) collective-permute-start(bf16[32,32,128]{2,1,0:T(8,128)(2,1)S(1)} %bitcast.44), channel_id=1, source_target_pairs={{0,128},{64,192},{128,0},{192,64},{1,129},{65,193},{129,1},{193,65... | collective-permute-start | bytes 786440 | tf_op jit(solution)/shard_map/ppermute | solution.py:282
  104.0 21.0 %collective-permute-start.24 = (bf16[32,32,128]{2,1,0:T(8,128)(2,1)S(1)}, bf16[32,32,128]{2,1,0:T(8,128)(2,1)S(1)}, u32[]{:S(2)}, u32[]{:S(2)}) collective-permute-start(bf16[32,32,128]{2,1,0:T(8,128)(2,1)S(1)} %bitcast.45), channel_id=1, source_target_pairs={{0,64},{64,0},{128,192},{192,128},{1,65},{65,1},{129,193},{193,129... | collective-permute-start | bytes 786440 | tf_op jit(solution)/shard_map/ppermute | solution.py:282
